TPU v7x, 128 devices: a whole 4x4x4 slice. The times are simulated.
128 devices in a mesh: req: 16 (over y, x), seq: 4 (over z), hid: 2 (over core).
Axes of the slice: x: 4, y: 4, z: 4, core: 2. Of those that a mesh axis runs over, the one named last changes fastest.
Arguments:
- tokens: bfloat16 [65536, 2048], P(('req', 'seq')), may hold values from -6 to 6
- attention_gain: bfloat16 [2048], replicated, may hold values from 0.099609375 to 1.8984375
- project_weight: bfloat16 [2048, 2048], P(None, 'hid'), may hold values from -0.125 to 0.125
- conv_weight: bfloat16 [4, 2048], P(None, 'hid'), may hold values from -3 to 3
- decay_down: bfloat16 [2048, 16], replicated, may hold values from -0.125 to 0.125
- decay_up: bfloat16 [16, 512], P(None, 'hid'), may hold values from -1.5 to 1.5
- decay_bias: float32 [512], P('hid'), may hold values from -2 to 10
- output_gate: bfloat16 [2048, 1024], P(None, 'hid'), may hold values from -0.125 to 0.125
- head_gain: bfloat16 [512], replicated, may hold values from 0.099609375 to 1.8984375
- output_weight: bfloat16 [1024, 2048], P('hid'), may hold values from -0.1875 to 0.1875
- mixer_gain: bfloat16 [2048], replicated, may hold values from 0.099609375 to 1.8984375
- gate_weight: bfloat16 [2048, 2816], P('req', 'hid'), may hold values from -0.125 to 0.125
- up_weight: bfloat16 [2048, 2816], P('req', 'hid'), may hold values from -0.125 to 0.125
- down_weight: bfloat16 [2816, 2048], P('hid', 'req'), may hold values from -0.109375 to 0.109375
- prompt_pages: int32 [16, 16], P('req'), may hold values from 0 to 64, as said below
- prompt_start: int32 [16, 16], P('req'), may hold values from 0 to 63, as said below
Outputs:
- hidden_out: bfloat16 [65536, 2048], P(('req', 'seq', 'hid'))
- page_states: bfloat16 [1024, 2, 256, 512], P(('req', 'seq'), 'hid')
- conv_edges: bfloat16 [1024, 3, 2048], P(('req', 'seq'), None, 'hid')
Inputs may be any that keep to these rules, and one draw needn't show every extreme that they name: `prompt_pages`: row r lists the page counts of the prompts of group r; 0 marks an unused slot; in every draw some group holds one prompt of all its 64 pages. `prompt_start`: the slots of a row that are used cover pages in increasing order without intersection and end by page 64; pages between prompts belong to none; an unused slot starts at page 64 - 1, and every draw has one.
All inputs are finite; a program needn't handle non-finite values.
Results may differ from a plain program's by a relative error of at most 0.014.
Values may be sent and summed in bfloat16 or wider, within the bound.
A program may use at most 192 MiB of HBM per device.

v0:
```python
import jax
import jax.numpy as jnp
from jax import lax
from jax.sharding import PartitionSpec as P

HK = 256
HV = 512
KCONV = 4
PAGE = 64
CONVW = 1024


EPSILON = 1e-06
TOP_PRECISION = lax.Precision.HIGHEST


def shifted(value, axis, steps):
    count = lax.axis_size(axis)
    first, last = (max(0, -steps), min(count, count - steps))
    return lax.ppermute(value, axis, [(source, source + steps) for source in range(first, last)])


def prefix_2(array, axis, join, neutral):
    place = lax.axis_index(axis)
    gathered = jax.tree.map(
        lambda a, kind: lax.all_gather(a.astype(kind), axis), array, (jnp.bfloat16, jnp.bfloat16)
    )
    state = jax.tree.map(lambda a, e: jnp.zeros_like(a) + jnp.asarray(e, a.dtype), array, neutral)

    def one(lap, state):
        return join(
            state,
            jax.tree.map(
                lambda a, own: lax.dynamic_index_in_dim(a, lap, 0, False).astype(own.dtype),
                gathered,
                array,
            ),
        )

    return lax.fori_loop(0, place, one, state)


def rms_scaled(values, scale_gain):
    values = values.astype(jnp.float32)
    return (
        values
        * lax.rsqrt(jnp.mean(values * values, axis=-1, keepdims=True) + EPSILON)
        * scale_gain.astype(jnp.float32)
    )


def page_segments(page_counts, starts, total_pages):
    position = jnp.arange(total_pages, dtype=jnp.int32)
    inside = (position[None, :] >= starts[:, None]) & (
        position[None, :] < starts[:, None] + page_counts[:, None]
    )
    labels = jnp.arange(1, page_counts.shape[0] + 1, dtype=jnp.int32)
    segment = jnp.sum(jnp.where(inside, labels[:, None], 0), axis=0) - 1
    earlier = jnp.concatenate([jnp.full((1,), -1, jnp.int32), segment[:-1]])
    return ((segment == earlier) & (segment >= 0)).astype(jnp.float32)


def short_conv(by_page, before, carried, conv_taps):
    kept_rows = before.astype(jnp.float32) * carried[:, None, None]
    widened = jnp.concatenate([kept_rows, by_page.astype(jnp.float32)], axis=1)
    tap_count = conv_taps.shape[0]
    length = by_page.shape[1]
    result = jnp.zeros(by_page.shape, jnp.float32)
    for offset in range(tap_count):
        result = (
            result
            + conv_taps[offset].astype(jnp.float32)
            * widened[:, tap_count - 1 - offset : tap_count - 1 - offset + length]
        )
    return result


def split_features(mixed_rows, key_width):
    query_rows = jax.nn.silu(mixed_rows[..., :key_width])
    key_rows = jax.nn.silu(mixed_rows[..., key_width : 2 * key_width]) * key_width ** (-0.5)
    value_matrix = mixed_rows[..., 2 * key_width :]
    return (
        query_rows.transpose(0, 2, 1, 3),
        key_rows.transpose(0, 2, 1, 3),
        value_matrix.transpose(0, 2, 1, 3),
    )


def page_step(memory_state, inputs):
    query_rows, key_rows, value_matrix, decay_sum, carried = inputs
    memory_state = memory_state * carried
    length = query_rows.shape[1]
    raised_rows = query_rows * jnp.exp(decay_sum)
    lowered = key_rows * jnp.exp(-decay_sum)
    scores = jnp.einsum("hik,hjk->hij", raised_rows, lowered, precision=TOP_PRECISION)
    rows_index = jnp.arange(length)
    causal = rows_index[:, None] >= rows_index[None, :]
    scores = jnp.where(causal[None], scores, 0.0)
    layer_output = jnp.einsum("hij,hjv->hiv", scores, value_matrix, precision=TOP_PRECISION)
    layer_output = layer_output + jnp.einsum(
        "eow,ews->eos", raised_rows, memory_state, precision=TOP_PRECISION
    )
    closing_sum = decay_sum[:, -1:, :]
    weighted_rows = key_rows * jnp.exp(closing_sum - decay_sum)
    memory_state = jnp.exp(closing_sum[:, 0, :])[:, :, None] * memory_state + jnp.einsum(
        "lte,ltb->leb", weighted_rows, value_matrix, precision=TOP_PRECISION
    )
    return (memory_state, (layer_output, memory_state))


def on_device(
    tokens,
    attention_gain,
    project_weight,
    conv_weight,
    decay_down,
    decay_up,
    decay_bias,
    output_gate,
    head_gain,
    output_weight,
    mixer_gain,
    gate_weight,
    up_weight,
    down_weight,
    prompt_pages,
    prompt_start,
):
    token_count = tokens.shape[0]
    page_count = token_count // PAGE
    local_heads = project_weight.shape[1] // CONVW
    rim_rows = KCONV - 1
    seq_index = lax.axis_index("seq")
    group_pages = page_count * lax.axis_size("seq")
    page_flags = page_segments(prompt_pages[0], prompt_start[0], group_pages)
    carried = lax.dynamic_slice_in_dim(page_flags, seq_index * page_count, page_count)
    normed = rms_scaled(tokens, attention_gain).astype(jnp.bfloat16)
    projected = jnp.dot(normed, project_weight, preferred_element_type=jnp.float32).astype(
        jnp.bfloat16
    )
    by_page = projected.reshape(page_count, PAGE, local_heads * CONVW)
    incoming = shifted(by_page[-1, PAGE - rim_rows :], "seq", 1)
    before = jnp.concatenate([incoming[None], by_page[:-1, PAGE - rim_rows :]], axis=0)
    mixed_rows = short_conv(by_page, before, carried, conv_weight).reshape(
        page_count, PAGE, local_heads, CONVW
    )
    query_rows, key_rows, value_matrix = split_features(mixed_rows, HK)
    lowrank = jnp.dot(normed, decay_down, preferred_element_type=jnp.float32).astype(jnp.bfloat16)
    decay_log = (
        jax.nn.log_sigmoid(
            jnp.dot(lowrank, decay_up, preferred_element_type=jnp.float32) + decay_bias
        )
        / 16.0
    )
    decay_log = decay_log.reshape(page_count, PAGE, local_heads, HK).transpose(0, 2, 1, 3)
    decay_sum = jnp.cumsum(decay_log, axis=2)
    start_memory = jnp.zeros((local_heads, HK, HV), jnp.float32)
    local_memory, (outputs, memories) = lax.scan(
        page_step, start_memory, (query_rows, key_rows, value_matrix, decay_sum, carried)
    )
    totals = decay_sum[:, :, -1, :]
    through = jnp.cumsum(totals, axis=0)
    alive_mask = jnp.cumprod(carried)
    block_decay = alive_mask[-1] * jnp.exp(through[-1])

    def compose(earlier, latter):
        return (earlier[0] * latter[0], latter[0][..., None] * earlier[1] + latter[1])

    prefix = prefix_2(
        (block_decay, local_memory),
        "seq",
        compose,
        (jnp.ones_like(block_decay), jnp.zeros_like(local_memory)),
    )
    incoming_state = prefix[1]
    before_sum = through - totals
    extent_factor = alive_mask[:, None, None, None] * jnp.exp(decay_sum + before_sum[:, :, None, :])
    outputs = outputs + jnp.einsum(
        "dlof,lfg->dlog", query_rows * extent_factor, incoming_state, precision=TOP_PRECISION
    )
    memories = (
        memories + (alive_mask[:, None, None] * jnp.exp(through))[..., None] * incoming_state[None]
    )
    attended = outputs.transpose(0, 2, 1, 3).reshape(token_count, local_heads, HV)
    normed_heads = rms_scaled(attended, head_gain)
    opening = jax.nn.silu(jnp.dot(normed, output_gate, preferred_element_type=jnp.float32)).reshape(
        token_count, local_heads, HV
    )
    gated_rows = (
        (normed_heads * opening).astype(jnp.bfloat16).reshape(token_count, local_heads * HV)
    )
    partial_value = jnp.dot(gated_rows, output_weight, preferred_element_type=jnp.float32)
    half_rows = token_count // lax.axis_size("hid")
    row_start = lax.axis_index("hid") * half_rows
    mixed_sum = lax.psum(partial_value.astype(jnp.bfloat16), "hid").astype(jnp.float32)
    residual = (tokens.astype(jnp.float32) + mixed_sum).astype(jnp.bfloat16)
    feed_in = rms_scaled(residual, mixer_gain).astype(jnp.bfloat16)
    own_residual = lax.dynamic_slice_in_dim(residual, row_start, half_rows, 0)

    def widen(weight_rows):
        return jnp.dot(feed_in, weight_rows, preferred_element_type=jnp.float32)

    gate_part = widen(lax.all_gather(gate_weight, "req", axis=0, tiled=True))
    up_part = widen(lax.all_gather(up_weight, "req", axis=0, tiled=True))
    hidden = (jax.nn.silu(gate_part) * up_part).astype(jnp.bfloat16)
    partials = jnp.dot(
        hidden,
        lax.all_gather(down_weight, "req", axis=1, tiled=True),
        preferred_element_type=jnp.float32,
    )
    feed_sum = lax.psum_scatter(
        partials.astype(jnp.bfloat16), "hid", scatter_dimension=0, tiled=True
    ).astype(jnp.float32)
    result = (own_residual.astype(jnp.float32) + feed_sum).astype(jnp.bfloat16)
    return (result, memories.astype(jnp.bfloat16), by_page[:, PAGE - rim_rows :])


def solution(mesh):
    return jax.shard_map(
        on_device,
        mesh=mesh,
        in_specs=(
            P(("req", "seq"), None),
            P(),
            P(None, "hid"),
            P(None, "hid"),
            P(),
            P(None, "hid"),
            P("hid"),
            P(None, "hid"),
            P(),
            P("hid", None),
            P(),
            P("req", "hid"),
            P("req", "hid"),
            P("hid", "req"),
            P("req", None),
            P("req", None),
        ),
        out_specs=(
            P(("req", "seq", "hid"), None),
            P(("req", "seq"), "hid", None, None),
            P(("req", "seq"), None, "hid"),
        ),
        check_vma=False,
    )
```

profile of v0, /device:TPU:1, one launch (start us, length us, event | category | flops | bytes accessed | tf_op | source)
XLA Modules:
  0.0 471.6 jit_solution(12928191912061938082)
XLA Ops:
  8.1 3.2 fusion.29
  11.6 7.2 %convolution_convert_fusion.2 = bf16[1024,1024]{1,0:T(8,128)(2,1)S(1)} fusion(bf16[2048,1024]{1,0:T(8,128)(2,1)} %param.22, bf16[1024,2048]{1,0:T(8,128)(2,1)S(1)} %copy-done.2, f32[2048]{0:T(1024)S(1)} %convert_element_type.146, f32[1024]{0:T(1024)S(1)} %add_rsqrt_fusion.2), kind=kOutput, calls=%fused_computation.78 | convolution fusion | flops 4304404480 | bytes 10498048 | tf_op jit(solution)/shard_map/dot_general | solution.py:138
  18.9 4.5 collective-permute-start
  23.5 3.2 copy_convert_fusion
  26.9 4.2 fusion.50
  34.4 7.3 %fusion.37 = f32[16,64,1,1024]{3,0,1,2:T(8,128)S(1)} fusion(f32[16,64,1024]{2,0,1:T(8,128)} %copy_convert_fusion, f32[16,3,1024]{2,0,1:T(8,128)S(1)} %convert_multiply_fusion.4, f32[1024]{0:T(1024)S(1)} %bitcast.168, f32[1024]{0:T(1024)S(1)} %bitcast.169, f32[1024]{0:T(1024)S(1)} %bitcast.167, f32[1024]{0:T(1024)S(1)} %bitcast.166), kind=kLoop, calls=%fused_computation.61 | loop fusion | flops 10485760 | bytes 8601600 | tf_op jit(solution)/shard_map/reshape | solution.py:144
  45.4 143.3 %while.28 = (s32[]{:T(128)}, f32[1,256,512]{2,1,0:T(8,128)S(1)}, f32[16,1,64,512]{3,2,1,0:T(8,128)}, f32[16,1,256,512]{3,2,1,0:T(8,128)}, f32[16,1,64,256]{3,0,1...) while((s32[]{:T(128)}, f32[1,256,512]{2,1,0:T(8,128)S(1)}, ...), condition=%wide.region_4.5_spmd.clone, body=%wide.region_3.4_spmd.clone.sunk | while | flops 240001024 | bytes 4038800 | solution.py:158
  70.1 2.2 bitcast_dynamic-update-slice_fusion.2
  141.7 2.2 bitcast_dynamic-update-slice_fusion.2
  190.8 6.9 %all_gather.19 = bf16[4,1,256]{2,1,0:T(2,128)(2,1)S(1)} all-gather(bf16[1,1,256]{2,1,0:T(2,128)(2,1)S(1)} %fusion.65), channel_id=1, replica_groups=mesh['req'=16,'seq'=4,'hid'=2] {'seq'}, dimensions={0}, use_global_device_ids=true | all-gather | bytes 2560 | tf_op jit(solution)/shard_map/all_gather | solution.py:26
  197.7 17.4 %all-gather.12.cloned.1.call-done = bf16[4,256,512]{2,1,0:T(8,128)(2,1)} async-done(((bf16[1,256,512]{2,1,0:T(8,128)(2,1)}), bf16[4,256,512]{2,1,0:T(8,128)(2,1)}) %all-gather.12.cloned.1.call-update) | async-done | bytes 1048592 | tf_op jit(solution)/shard_map/all_gather | solution.py:26
  215.4 5.6 %multiply_reduce_fusion = (f32[16,64]{1,0:T(8,128)S(1)}, f32[16,1,64,512]{3,2,0,1:T(8,128)}) fusion(f32[16,64,256]{2,0,1:T(8,128)} %get-tuple-element.223, f32[1,256,512]{2,1,0:T(8,128)S(1)} %get-tuple-element.98, f32[16,1,64,512]{3,2,1,0:T(8,128)} %get-tuple-element.96), kind=kOutput, calls=%fused_computation.77 | convolution fusion | flops 1612184576 | bytes 5771264 | tf_op jit(solution)/shard_map/dlof,lfg->dlog/dot_general | solution.py:178
  221.1 6.2 %fusion.44 = bf16[1024,512]{1,0:T(8,128)(2,1)S(1)} fusion(f32[16,1,64,512]{3,2,0,1:T(8,128)} %get-tuple-element.231, f32[512]{0:T(512)S(1)} %convert_element_type.163, f32[1024]{0:T(1024)S(1)} %rsqrt.29, bf16[2048,512]{1,0:T(8,128)(2,1)} %param.27, bf16[1024,2048]{1,0:T(8,128)(2,1)} %param.20, f32[2048]{0:T(1024)S(1)} %convert_element_type.146, ...), kind=kOutput, calls=%fused_computation.76 | convolution fusion | flops 2160066560 | bytes 9455616 | tf_op jit(solution)/shard_map/dot_general | solution.py:186
  227.2 4.4 convolution_convert_fusion.1
  233.7 36.6 %all-reduce.2.cloned.1.call-done = bf16[1024,2048]{1,0:T(8,128)(2,1)} async-done(((bf16[1024,2048]{1,0:T(8,128)(2,1)}), bf16[1024,2048]{1,0:T(8,128)(2,1)}) %all-reduce.2.cloned.1.call-update) | async-done | bytes 4194320 | tf_op jit(solution)/shard_map/psum | solution.py:195
  270.3 7.7 %fusion.26 = (f32[1024]{0:T(1024)S(1)}, bf16[1024,2048]{1,0:T(8,128)(2,1)}) fusion(bf16[1024,2048]{1,0:T(8,128)(2,1)} %all-reduce.2.cloned.1.call-done, bf16[1024,2048]{1,0:T(8,128)(2,1)} %param.20), kind=kLoop, calls=%fused_computation.44 | loop fusion | flops 14679040 | bytes 12587008 | tf_op jit(solution)/shard_map/reduce_sum | solution.py:47
  278.0 19.1 %all-gather.6.cloned.1.call-done = bf16[2048,1408]{1,0:T(8,128)(2,1)} async-done(((bf16[128,1408]{1,0:T(8,128)(2,1)}), bf16[2048,1408]{1,0:T(8,128)(2,1)}) %all-gather.6.cloned.1.call-update) | async-done | bytes 5767184 | tf_op jit(solution)/shard_map/all_gather | solution.py:203
  297.1 12.0 %fusion.47 = f32[1024,1408]{1,0:T(8,128)} fusion(bf16[2048,1408]{1,0:T(8,128)(2,1)} %all-gather.6.cloned.1.call-done, bf16[1024,2048]{1,0:T(8,128)(2,1)} %get-tuple-element.218, f32[2048]{0:T(1024)S(1)} %convert_element_type.170, f32[1024]{0:T(1024)S(1)} %add_rsqrt_fusion.1), kind=kOutput, calls=%fused_computation.81 | convolution fusion | flops 5913968640 | bytes 15740928 | tf_op jit(solution)/shard_map/dot_general | solution.py:201
  309.0 53.5 %all-gather.10.cloned.1.call-done = bf16[1408,2048]{1,0:T(8,128)(2,1)} async-done(((bf16[1408,128]{1,0:T(8,128)(2,1)}), bf16[1408,2048]{1,0:T(8,128)(2,1)}) %all-gather.10.cloned.1.call-update) | async-done | bytes 5767184 | tf_op jit(solution)/shard_map/all_gather | solution.py:208
  362.5 61.3 %all-gather.8.cloned.1.call-done = bf16[2048,1408]{1,0:T(8,128)(2,1)} async-done(((bf16[128,1408]{1,0:T(8,128)(2,1)}), bf16[2048,1408]{1,0:T(8,128)(2,1)}) %all-gather.8.cloned.1.call-update) | async-done | bytes 5767184 | tf_op jit(solution)/shard_map/all_gather | solution.py:204
  423.8 20.9 %convolution_convert_fusion = bf16[1024,2048]{1,0:T(8,128)(2,1)} fusion(bf16[1408,2048]{1,0:T(8,128)(2,1)} %all-gather.10.cloned.1.call-done, f32[1024,1408]{1,0:T(8,128)} %fusion.47, bf16[2048,1408]{1,0:T(8,128)(2,1)} %all-gather.8.cloned.1.call-done, bf16[1024,2048]{1,0:T(8,128)(2,1)} %get-tuple-element.218, f32[2048]{0:T(1024)S(1)} %convert_element_type.170, ...), kind=kOutput, calls=%fused_computation.68 | convolution fusion | flops 11830296576 | bytes 25702400 | tf_op jit(solution)/shard_map/dot_general | solution.py:206
  446.5 5.4 %add_convert_fusion = bf16[16,1,256,512]{3,2,1,0:T(8,128)(2,1)} fusion(f32[16,1,256,512]{3,2,1,0:T(8,128)} %get-tuple-element.99, f32[256,512]{1,0:T(8,128)S(1)} %bitcast.155, f32[16,256]{1,0:T(8,128)S(1)} %bitcast_multiply_fusion.1), kind=kLoop, calls=%fused_computation.51 | loop fusion | flops 6291456 | bytes 13123584 | tf_op jit(solution)/shard_map/convert_element_type | solution.py:215
  451.8 7.9 %reduce-scatter.2.cloned.1.call-done = bf16[512,2048]{1,0:T(8,128)(2,1)} async-done(((bf16[1024,2048]{1,0:T(8,128)(2,1)}), bf16[512,2048]{1,0:T(8,128)(2,1)}) %reduce-scatter.2.cloned.1.call-update) | async-done | bytes 2097168 | tf_op jit(solution)/shard_map/reduce_scatter | solution.py:211
  459.8 4.4 add_convert_fusion.1
  (256 shorter events, 152.0 us)
Async XLA Ops:
  8.0 219.2 %copy-start = (bf16[512,2048]{1,0:T(8,128)(2,1)S(1)}, bf16[512,2048]{1,0:T(8,128)(2,1)}, u32[]{:S(2)}) copy-start(bf16[512,2048]{1,0:T(8,128)(2,1)} %param.29) | copy-start | bytes 6291460
  8.0 3.3 copy-start.7
  8.0 207.1 %all-gather.12.cloned.1.call-start = ((), (), s32[]{:S(2)}) async-start(), calls=%async_computation.6 | async-start | bytes 1310720 | tf_op jit(solution)/shard_map/all_gather | solution.py:26
  8.1 3.6 copy-start.2
  18.8 4.6 copy-start.5
  18.8 7.8 %copy-start.9 = (s32[1,16]{1,0:T(1,128)S(1)}, s32[1,16]{1,0:T(1,128)}, u32[]{:S(2)}) copy-start(s32[1,16]{1,0:T(1,128)} %param.35) | copy-start | bytes 196
  18.9 7.8 %copy-start.11 = (s32[1,16]{1,0:T(1,128)S(1)}, s32[1,16]{1,0:T(1,128)}, u32[]{:S(2)}) copy-start(s32[1,16]{1,0:T(1,128)} %param.34) | copy-start | bytes 196
  18.9 7.9 %copy-start.6 = (bf16[4,1024]{1,0:T(4,128)(2,1)S(1)}, bf16[4,1024]{1,0:T(4,128)(2,1)}, u32[]{:S(2)}) copy-start(bf16[4,1024]{1,0:T(4,128)(2,1)} %param.23) | copy-start | bytes 24580
  18.9 8.0 %copy-start.12 = (bf16[2048,16]{0,1:T(8,128)(2,1)S(1)}, bf16[2048,16]{0,1:T(8,128)(2,1)}, u32[]{:S(2)}) copy-start(bf16[2048,16]{0,1:T(8,128)(2,1)} %param.24) | copy-start | bytes 196612
  18.9 8.0 %copy-start.13 = (bf16[16,256]{1,0:T(8,128)(2,1)S(1)}, bf16[16,256]{1,0:T(8,128)(2,1)}, u32[]{:S(2)}) copy-start(bf16[16,256]{1,0:T(8,128)(2,1)} %param.25) | copy-start | bytes 24580
  18.9 7.9 %copy-start.14 = (f32[256]{0:T(256)S(1)}, f32[256]{0:T(256)}, u32[]{:S(2)}) copy-start(f32[256]{0:T(256)} %param.26) | copy-start | bytes 3076
  18.9 15.4 %collective-permute-start = (bf16[3,1024]{1,0:T(4,128)(2,1)S(1)}, bf16[3,1024]{1,0:T(4,128)(2,1)S(1)}, u32[]{:S(2)}, u32[]{:S(2)}) collective-permute-start(bf16[3,1024]{1,0:T(4,128)(2,1)S(1)} %slice_bitcast_fusion.2), channel_id=1, source_target_pairs={{0,2},{2,4},{4,6},{1,3},{3,5},{5,7},{8,10},{10,12},{12,14},{9,11},... | collective-permute-start | bytes 18440 | tf_op jit(solution)/shard_map/ppermute | solution.py:20
  31.7 1.0 copy-start.3
  41.7 1.6 copy-start.4
  45.4 144.7 %copy-start.10 = (bf16[512]{0:T(512)(128)(2,1)S(1)}, bf16[512]{0:T(512)(128)(2,1)}, u32[]{:S(2)}) copy-start(bf16[512]{0:T(512)(128)(2,1)} %param.28) | copy-start | bytes 3076
  189.5 80.8 %all-reduce.2.cloned.1.call-start = ((), (), s32[]{:S(2)}) async-start(), calls=%async_computation.1 | async-start | bytes 8388608 | tf_op jit(solution)/shard_map/psum | solution.py:195
  231.6 2.0 copy-start.8
  231.6 65.5 %all-gather.6.cloned.1.call-start = ((), (), s32[]{:S(2)}) async-start(), calls=%async_computation.2 | async-start | bytes 6127616 | tf_op jit(solution)/shard_map/all_gather | solution.py:203
  232.2 130.3 %all-gather.10.cloned.1.call-start = ((), (), s32[]{:S(2)}) async-start(), calls=%async_computation.4 | async-start | bytes 6127616 | tf_op jit(solution)/shard_map/all_gather | solution.py:208
  232.8 191.0 %all-gather.8.cloned.1.call-start = ((), (), s32[]{:S(2)}) async-start(), calls=%async_computation.3 | async-start | bytes 6127616 | tf_op jit(solution)/shard_map/all_gather | solution.py:204
  233.4 226.4 %reduce-scatter.2.cloned.1.call-start = ((), (), s32[]{:S(2)}) async-start(), calls=%async_computation.5 | async-start | bytes 6291456 | tf_op jit(solution)/shard_map/reduce_scatter | solution.py:211
  446.5 17.8 %copy-start.1 = (bf16[512,2048]{1,0:T(8,128)(2,1)S(1)}, bf16[512,2048]{1,0:T(8,128)(2,1)}, u32[]{:S(2)}) copy-start(bf16[512,2048]{1,0:T(8,128)(2,1)} %param.29) | copy-start | bytes 6291460
Sparse Core Ops, SparseCore 0:
  189.6 25.4 all-gather.11
  231.7 38.5 all-reduce.1
  444.8 14.9 reduce-scatter.1
Sparse Core Ops, SparseCore 1:
  234.4 62.6 all-gather.5
  299.3 63.2 all-gather.9
  364.7 59.0 all-gather.7
where the time goes:
time: 474 us; the launch traced here: 472 us
  waiting for transfers between devices  197 us (42%)
  matrix products  132 us (28%)
  local copies, waits for them, and re-layouts  77.3 us (16%)
  other arithmetic  36 us (8%)
  between operations  15.8 us (3%)
  blocking collectives  6.89 us (1%)
  starting transfers between devices  4.97 us (1%)
    dynamic_slice x80, local copies, waits for them, and re-layouts, on_device(): lax.scan(page_step, start_memory, (query_rows, key_rows, value_matrix, de...  70.5 us
    all_gather x1, waiting for transfers between devices, on_device(): up_part = widen(lax.all_gather(up_weight, 'req', axis=0, tiled=True))  61.3 us
    all_gather x1, waiting for transfers between devices, on_device(): lax.all_gather(down_weight, 'req', axis=1, tiled=True)  53.5 us
    psum x1, waiting for transfers between devices, on_device(): lax.psum(partial_value.astype(jnp.bfloat16), 'hid').astype(jnp.float32)  36.6 us
    dot_general x16, matrix products, page_step(): jnp.einsum('lte,ltb->leb', weighted_rows, value_matrix, precision=TOP_PRE...  35.4 us
    dot_general x16, matrix products, page_step(): jnp.einsum('eow,ews->eos', raised_rows, memory_state, precision=TOP_PRECI...  29 us
    dot_general x1, matrix products, on_device(): jnp.dot(hidden, lax.all_gather(down_weight, 'req', axis=1, tiled=True), p...  20.9 us
    all_gather x1, waiting for transfers between devices, on_device(): gate_part = widen(lax.all_gather(gate_weight, 'req', axis=0, tiled=True))  19.1 us
  transfers between devices with their start and end apart: 7, of which 6 were waited for; matrix products, arithmetic and copies ran while one was open for 8% of the time, Pallas kernels for 0%

commit v1 on v0

--- a/solution.py
+++ b/solution.py
@@ -86,26 +86,35 @@
     )
 
 
-def page_step(memory_state, inputs):
-    query_rows, key_rows, value_matrix, decay_sum, carried = inputs
-    memory_state = memory_state * carried
-    length = query_rows.shape[1]
+def page_block(query_rows, key_rows, value_matrix, decay_sum, carried):
+    length = query_rows.shape[2]
+    page_count = query_rows.shape[0]
     raised_rows = query_rows * jnp.exp(decay_sum)
     lowered = key_rows * jnp.exp(-decay_sum)
-    scores = jnp.einsum("hik,hjk->hij", raised_rows, lowered, precision=TOP_PRECISION)
+    scores = jnp.einsum("phik,phjk->phij", raised_rows, lowered, precision=TOP_PRECISION)
     rows_index = jnp.arange(length)
     causal = rows_index[:, None] >= rows_index[None, :]
-    scores = jnp.where(causal[None], scores, 0.0)
-    layer_output = jnp.einsum("hij,hjv->hiv", scores, value_matrix, precision=TOP_PRECISION)
+    scores = jnp.where(causal[None, None], scores, 0.0)
+    layer_output = jnp.einsum("phij,phjv->phiv", scores, value_matrix, precision=TOP_PRECISION)
+    closing_sum = decay_sum[:, :, -1, :]
+    weighted_rows = key_rows * jnp.exp(closing_sum[:, :, None, :] - decay_sum)
+    page_terms = jnp.einsum(
+        "phte,phtb->pheb", weighted_rows, value_matrix, precision=TOP_PRECISION
+    )
+    through = jnp.cumsum(closing_sum, axis=0)
+    resets = jnp.cumsum(1.0 - carried)
+    pages = jnp.arange(page_count)
+    valid = (pages[:, None] >= pages[None, :]) & (resets[:, None] == resets[None, :])
+    spread = through[:, None] - through[None, :]
+    spread = jnp.where(valid[:, :, None, None], spread, 0.0)
+    weights = jnp.where(valid[:, :, None, None], jnp.exp(spread), 0.0)
+    memories = jnp.einsum("pqhe,qheb->pheb", weights, page_terms, precision=TOP_PRECISION)
+    previous = jnp.concatenate([jnp.zeros_like(memories[:1]), memories[:-1]], axis=0)
+    previous = previous * carried[:, None, None, None]
     layer_output = layer_output + jnp.einsum(
-        "eow,ews->eos", raised_rows, memory_state, precision=TOP_PRECISION
-    )
-    closing_sum = decay_sum[:, -1:, :]
-    weighted_rows = key_rows * jnp.exp(closing_sum - decay_sum)
-    memory_state = jnp.exp(closing_sum[:, 0, :])[:, :, None] * memory_state + jnp.einsum(
-        "lte,ltb->leb", weighted_rows, value_matrix, precision=TOP_PRECISION
-    )
-    return (memory_state, (layer_output, memory_state))
+        "phik,phkv->phiv", raised_rows, previous, precision=TOP_PRECISION
+    )
+    return memories[-1], layer_output, memories
 
 
 def on_device(
@@ -154,9 +163,8 @@
     )
     decay_log = decay_log.reshape(page_count, PAGE, local_heads, HK).transpose(0, 2, 1, 3)
     decay_sum = jnp.cumsum(decay_log, axis=2)
-    start_memory = jnp.zeros((local_heads, HK, HV), jnp.float32)
-    local_memory, (outputs, memories) = lax.scan(
-        page_step, start_memory, (query_rows, key_rows, value_matrix, decay_sum, carried)
+    local_memory, outputs, memories = page_block(
+        query_rows, key_rows, value_matrix, decay_sum, carried
     )
     totals = decay_sum[:, :, -1, :]
     through = jnp.cumsum(totals, axis=0)

time: 474 us -> 371 us (0.78)
  local copies, waits for them, and re-layouts: 77.3 us -> 14.4 us
  matrix products: 132 us -> 104 us
  waiting for transfers between devices: 197 us -> 178 us
    dynamic_slice x81 -> x0, local copies, waits for them, and re-layouts: 70.5 us -> none  [the longest x80 70.5 us: on_device(): lax.scan(page_step, start_memory, (query_rows, key_rows, value_matrix, de...]
    dot_general x64 -> x5, matrix products: 72.1 us -> 41.4 us  [the longest x1 13.6 us: page_block(): jnp.einsum('pqhe,qheb->pheb', weights, page_terms, precision=TOP_PRECISION)]
    all_gather x1, waiting for transfers between devices: 17.4 us -> 0.01 us  [prefix_2(): lax.all_gather(a.astype(kind), axis)]
    unnamed x32 -> x37, local copies, waits for them, and re-layouts: 2.03 us -> 10.1 us
    another operation x3 -> x7, other arithmetic: 0.19 us -> 5.75 us
  transfers between devices with their start and end apart: 7 -> 7, of which waited for: 6 -> 5; matrix products, arithmetic and copies ran while one was open for 8% -> 19% of each run, Pallas kernels for 0% -> 0%
where the time goes in v1:
time: 371 us; the launch traced here: 364 us
  waiting for transfers between devices  178 us (48%)
  matrix products  104 us (28%)
  other arithmetic  39.8 us (11%)
  between operations  16.3 us (4%)
  local copies, waits for them, and re-layouts  14.4 us (4%)
  blocking collectives  6.9 us (2%)
  starting transfers between devices  5.04 us (1%)
    all_gather x1, waiting for transfers between devices, on_device(): up_part = widen(lax.all_gather(up_weight, 'req', axis=0, tiled=True))  61.3 us
    all_gather x1, waiting for transfers between devices, on_device(): lax.all_gather(down_weight, 'req', axis=1, tiled=True)  53.5 us
    psum x1, waiting for transfers between devices, on_device(): lax.psum(partial_value.astype(jnp.bfloat16), 'hid').astype(jnp.float32)  37.7 us
    dot_general x1, matrix products, on_device(): jnp.dot(hidden, lax.all_gather(down_weight, 'req', axis=1, tiled=True), p...  20.9 us
    all_gather x1, waiting for transfers between devices, on_device(): gate_part = widen(lax.all_gather(gate_weight, 'req', axis=0, tiled=True))  19.1 us
    dot_general x1, matrix products, page_block(): jnp.einsum('pqhe,qheb->pheb', weights, page_terms, precision=TOP_PRECISION)  13.6 us
    dot_general x1, matrix products, page_block(): jnp.einsum('phik,phkv->phiv', raised_rows, previous, precision=TOP_PRECIS...  13.1 us
    dot_general x1, matrix products, widen(): return jnp.dot(feed_in, weight_rows, preferred_element_type=jnp.float32)  12 us
  transfers between devices with their start and end apart: 7, of which 5 were waited for; matrix products, arithmetic and copies ran while one was open for 19% of the time, Pallas kernels for 0%

profile of v1, /device:TPU:1, one launch (start us, length us, event | category | flops | bytes accessed | tf_op | source)
XLA Modules:
  0.0 364.4 jit_solution(5683534701682440027)
XLA Ops:
  11.7 7.3 %convolution_convert_fusion.2 = bf16[1024,1024]{1,0:T(8,128)(2,1)S(1)} fusion(bf16[2048,1024]{1,0:T(8,128)(2,1)} %param.20, bf16[1024,2048]{1,0:T(8,128)(2,1)S(1)} %copy-done.6, f32[2048]{0:T(1024)S(1)} %convert_element_type.149, f32[1024]{0:T(1024)S(1)} %add_rsqrt_fusion.2), kind=kOutput, calls=%fused_computation.53 | convolution fusion | flops 4304404480 | bytes 10498048 | tf_op jit(solution)/shard_map/dot_general | solution.py:147
  20.3 4.4 %collective-permute-start = (bf16[3,1024]{1,0:T(4,128)(2,1)S(1)}, bf16[3,1024]{1,0:T(4,128)(2,1)S(1)}, u32[]{:S(2)}, u32[]{:S(2)}) collective-permute-start(bf16[3,1024]{1,0:T(4,128)(2,1)S(1)} %slice_bitcast_fusion.5), channel_id=1, source_target_pairs={{0,2},{2,4},{4,6},{1,3},{3,5},{5,7},{8,10},{10,12},{12,14},{9,11},... | collective-permute-start | bytes 18440 | tf_op jit(solution)/shard_map/ppermute | solution.py:20
  24.9 5.2 %fusion.37 = f32[1024,256]{1,0:T(8,128)} fusion(bf16[16,256]{1,0:T(8,128)(2,1)S(1)} %copy-done.15, bf16[2048,16]{0,1:T(8,128)(2,1)S(1)} %copy-done.14, f32[256]{0:T(256)S(1)} %copy-done.16, bf16[1024,2048]{1,0:T(8,128)(2,1)} %param.18, f32[2048]{0:T(1024)S(1)} %convert_element_type.149, f32[1024]{0:T(1024)S(1)} %add_rsqrt_fusion.2), kind=kOutput, calls=%fused_computation.60 | convolution fusion | flops 86523904 | bytes 5329920 | tf_op jit(solution)/shard_map/dot_general | solution.py:160
  34.8 4.1 %convert_element_type.152 = f32[16,64,1024]{2,1,0:T(8,128)} convert(bf16[16,64,1024]{2,1,0:T(8,128)(2,1)} %bitcast.138) | non-fusion elementwise | flops 1048576 | bytes 6291456 | tf_op jit(solution)/shard_map/convert_element_type | solution.py:65
  39.1 6.9 %all_gather.17 = bf16[4,1,256]{2,1,0:T(2,128)(2,1)S(1)} all-gather(bf16[1,1,256]{2,1,0:T(2,128)(2,1)S(1)} %fusion.71), channel_id=1, replica_groups=mesh['req'=16,'seq'=4,'hid'=2] {'seq'}, dimensions={0}, use_global_device_ids=true | all-gather | bytes 2560 | tf_op jit(solution)/shard_map/all_gather | solution.py:26
  46.1 7.6 %fusion.15 = f32[16,64,1,1024]{3,1,0,2:T(8,128)S(1)} fusion(f32[16,64,1024]{2,1,0:T(8,128)} %convert_element_type.152, f32[16,3,1024]{2,1,0:T(4,128)S(1)} %convert_multiply_fusion.4, f32[1024]{0:T(1024)S(1)} %bitcast.145, f32[1024]{0:T(1024)S(1)} %bitcast.146, f32[1024]{0:T(1024)S(1)} %bitcast.144, f32[1024]{0:T(1024)S(1)} %bitcast.143), kind=kLoop, calls=%fused_computation.29 | loop fusion | flops 10485760 | bytes 8601600 | tf_op jit(solution)/shard_map/reshape | solution.py:153
  53.7 7.4 %fusion.30 = f32[16,256,512]{2,1,0:T(8,128)S(1)} fusion(f32[16,64,1,1024]{3,1,0,2:T(8,128)S(1)} %fusion.15, f32[16,1,64,256]{3,0,1,2:T(8,128)S(1)} %fusion.48, f32[16,256]{1,0:T(8,128)S(1)} %get-tuple-element.85), kind=kOutput, calls=%fused_computation.51 | convolution fusion | flops 1612447744 | bytes 12599296 | tf_op jit(solution)/shard_map/phte,phtb->pheb/dot_general | solution.py:101
  61.1 13.6 %fusion.20 = f32[16,1,256,512]{3,0,2,1:T(8,128)S(1)} fusion(f32[16,256,512]{2,1,0:T(8,128)S(1)} %fusion.30, f32[16,256]{0,1:T(8,128)S(1)} %bitcast.140, pred[16,16]{1,0:T(8,128)(4,1)S(1)} %fusion.69), kind=kOutput, calls=%fused_computation.38 | convolution fusion | flops 402849792 | bytes 16793856 | tf_op jit(solution)/shard_map/pqhe,qheb->pheb/dot_general | solution.py:111
  79.5 4.2 %convolution_select_fusion = f32[16,64,64]{2,1,0:T(8,128)S(1)} fusion(f32[16,1,64,256]{3,0,1,2:T(8,128)S(1)} %fusion.48, pred[64,64]{1,0:T(8,128)(4,1)S(1)} %iota_compare_fusion, f32[16,64,1,1024]{3,1,0,2:T(8,128)} %copy-done.3), kind=kOutput, calls=%fused_computation.56 | convolution fusion | flops 204537856 | bytes 4464640 | tf_op jit(solution)/shard_map/phik,phjk->phij/dot_general | solution.py:94
  86.9 5.3 %multiply_bitcast_fusion = f32[16,256,512]{2,0,1:T(8,128)S(1)} fusion(f32[15,1,256,512]{3,0,2,1:T(8,128)} %bitcast.134, f32[16]{0:T(128)S(1)} %get-tuple-element.83), kind=kLoop, calls=%fused_computation.19 | loop fusion | flops 2097152 | bytes 16252992 | tf_op jit(solution)/shard_map/reshape.33
  92.3 13.1 %fusion.7 = f32[16,64,512]{2,1,0:T(8,128)} fusion(f32[16,256,512]{2,0,1:T(8,128)S(1)} %multiply_bitcast_fusion, f32[16,1,64,256]{3,0,1,2:T(8,128)S(1)} %fusion.48, f32[16,64,1,1024]{3,1,0,2:T(8,128)} %copy-done.3), kind=kOutput, calls=%fused_computation.14 | convolution fusion | flops 1611923456 | bytes 12582912 | tf_op jit(solution)/shard_map/phik,phkv->phiv/dot_general | solution.py:114
  105.5 6.8 %multiply_reduce_fusion = (f32[16,64]{1,0:T(8,128)S(1)}, f32[16,1,64,512]{3,2,0,1:T(8,128)}) fusion(f32[16,1,64,256]{3,0,1,2:T(8,128)} %copy-done.5, f32[16,256]{1,0:T(8,128)S(1)} %get-tuple-element.84, f32[16]{0:T(128)S(1)} %reduce.3, f32[16,64,1,1024]{3,1,0,2:T(8,128)} %copy-done.3, f32[1,256,512]{2,1,0:T(8,128)S(1)} %get-tuple-element.47, ...), kind=kOutput, calls=%fused_computation.46 | convolution fusion | flops 1614543872 | bytes 8933440 | tf_op jit(solution)/shard_map/dlof,lfg->dlog/dot_general | solution.py:186
  112.4 6.2 %fusion.25 = bf16[1024,512]{1,0:T(8,128)(2,1)S(1)} fusion(f32[16,1,64,512]{3,2,0,1:T(8,128)} %get-tuple-element.91, f32[512]{0:T(512)S(1)} %convert_element_type.163, f32[1024]{0:T(1024)S(1)} %rsqrt.29, bf16[2048,512]{1,0:T(8,128)(2,1)} %param.25, bf16[1024,2048]{1,0:T(8,128)(2,1)} %param.18, f32[2048]{0:T(1024)S(1)} %convert_element_type.149, ...), kind=kOutput, calls=%fused_computation.45 | convolution fusion | flops 2160066560 | bytes 9455616 | tf_op jit(solution)/shard_map/dot_general | solution.py:194
  118.5 4.4 %convolution_convert_fusion.1 = bf16[1024,2048]{1,0:T(8,128)(2,1)} fusion(bf16[1024,512]{1,0:T(8,128)(2,1)S(1)} %fusion.25, bf16[512,2048]{1,0:T(8,128)(2,1)S(1)} %copy-done), kind=kOutput, calls=%fused_computation.37 | convolution fusion | flops 2149580800 | bytes 7340032 | tf_op jit(solution)/shard_map/dot_general | solution.py:200
  125.0 37.7 %all-reduce.3.cloned.1.call-done = bf16[1024,2048]{1,0:T(8,128)(2,1)} async-done(((bf16[1024,2048]{1,0:T(8,128)(2,1)}), bf16[1024,2048]{1,0:T(8,128)(2,1)}) %all-reduce.3.cloned.1.call-update) | async-done | bytes 4194320 | tf_op jit(solution)/shard_map/psum | solution.py:203
  162.7 7.7 %fusion = (f32[1024]{0:T(1024)S(1)}, bf16[1024,2048]{1,0:T(8,128)(2,1)}) fusion(bf16[1024,2048]{1,0:T(8,128)(2,1)} %all-reduce.3.cloned.1.call-done, bf16[1024,2048]{1,0:T(8,128)(2,1)} %param.18), kind=kLoop, calls=%fused_computation.7 | loop fusion | flops 14679040 | bytes 12587008 | tf_op jit(solution)/shard_map/reduce_sum | solution.py:47
  170.4 19.1 %all-gather.7.cloned.1.call-done = bf16[2048,1408]{1,0:T(8,128)(2,1)} async-done(((bf16[128,1408]{1,0:T(8,128)(2,1)}), bf16[2048,1408]{1,0:T(8,128)(2,1)}) %all-gather.7.cloned.1.call-update) | async-done | bytes 5767184 | tf_op jit(solution)/shard_map/all_gather | solution.py:211
  189.4 12.0 %fusion.34 = f32[1024,1408]{1,0:T(8,128)} fusion(bf16[2048,1408]{1,0:T(8,128)(2,1)} %all-gather.7.cloned.1.call-done, bf16[1024,2048]{1,0:T(8,128)(2,1)} %get-tuple-element.81, f32[2048]{0:T(1024)S(1)} %convert_element_type.170, f32[1024]{0:T(1024)S(1)} %add_rsqrt_fusion.1), kind=kOutput, calls=%fused_computation.57 | convolution fusion | flops 5913968640 | bytes 15740928 | tf_op jit(solution)/shard_map/dot_general | solution.py:209
  201.4 53.5 %all-gather.11.cloned.1.call-done = bf16[1408,2048]{1,0:T(8,128)(2,1)} async-done(((bf16[1408,128]{1,0:T(8,128)(2,1)}), bf16[1408,2048]{1,0:T(8,128)(2,1)}) %all-gather.11.cloned.1.call-update) | async-done | bytes 5767184 | tf_op jit(solution)/shard_map/all_gather | solution.py:216
  254.9 61.3 %all-gather.9.cloned.1.call-done = bf16[2048,1408]{1,0:T(8,128)(2,1)} async-done(((bf16[128,1408]{1,0:T(8,128)(2,1)}), bf16[2048,1408]{1,0:T(8,128)(2,1)}) %all-gather.9.cloned.1.call-update) | async-done | bytes 5767184 | tf_op jit(solution)/shard_map/all_gather | solution.py:212
  316.1 20.9 %convolution_convert_fusion = bf16[1024,2048]{1,0:T(8,128)(2,1)} fusion(bf16[1408,2048]{1,0:T(8,128)(2,1)} %all-gather.11.cloned.1.call-done, f32[1024,1408]{1,0:T(8,128)} %fusion.34, bf16[2048,1408]{1,0:T(8,128)(2,1)} %all-gather.9.cloned.1.call-done, bf16[1024,2048]{1,0:T(8,128)(2,1)} %get-tuple-element.81, f32[2048]{0:T(1024)S(1)} %convert_element_type.170, ...), kind=kOutput, calls=%fused_computation.36 | convolution fusion | flops 11830296576 | bytes 25702400 | tf_op jit(solution)/shard_map/dot_general | solution.py:214
  342.9 4.4 %copy.71 = bf16[16,1,256,512]{3,2,1,0:T(8,128)(2,1)} copy(bf16[16,1,256,512]{3,0,2,1:T(8,128)(2,1)S(1)} %add_convert_fusion) | data formatting | bytes 8388608
  347.3 4.8 %reduce-scatter.2.cloned.1.call-done = bf16[512,2048]{1,0:T(8,128)(2,1)} async-done(((bf16[1024,2048]{1,0:T(8,128)(2,1)}), bf16[512,2048]{1,0:T(8,128)(2,1)}) %reduce-scatter.2.cloned.1.call-update) | async-done | bytes 2097168 | tf_op jit(solution)/shard_map/reduce_scatter | solution.py:219
  352.1 4.4 %add_convert_fusion.1 = bf16[512,2048]{1,0:T(8,128)(2,1)} fusion(bf16[512,2048]{1,0:T(8,128)(2,1)} %reduce-scatter.2.cloned.1.call-done, bf16[1024,2048]{1,0:T(8,128)(2,1)} %get-tuple-element.81, s32[]{:T(128)S(6)} %select_n.46), kind=kLoop, calls=%fused_computation.35 | loop fusion | flops 4194304 | bytes 6291460 | tf_op jit(solution)/shard_map/convert_element_type | solution.py:222
  (90 shorter events, 26.0 us)
Async XLA Ops:
  8.0 110.5 %copy-start = (bf16[512,2048]{1,0:T(8,128)(2,1)S(1)}, bf16[512,2048]{1,0:T(8,128)(2,1)}, u32[]{:S(2)}) copy-start(bf16[512,2048]{1,0:T(8,128)(2,1)} %param.27) | copy-start | bytes 6291460
  8.0 3.3 copy-start.9
  8.0 97.4 %all-gather.5.cloned.1.call-start = ((), (), s32[]{:S(2)}) async-start(), calls=%async_computation.1 | async-start | bytes 1310720 | tf_op jit(solution)/shard_map/all_gather | solution.py:26
  8.1 3.6 copy-start.6
  11.6 13.0 %copy-start.11 = (s32[1,16]{1,0:T(1,128)S(1)}, s32[1,16]{1,0:T(1,128)}, u32[]{:S(2)}) copy-start(s32[1,16]{1,0:T(1,128)} %param.33) | copy-start | bytes 196
  11.6 13.0 %copy-start.13 = (s32[1,16]{1,0:T(1,128)S(1)}, s32[1,16]{1,0:T(1,128)}, u32[]{:S(2)}) copy-start(s32[1,16]{1,0:T(1,128)} %param.32) | copy-start | bytes 196
  11.6 13.2 %copy-start.8 = (bf16[4,1024]{1,0:T(4,128)(2,1)S(1)}, bf16[4,1024]{1,0:T(4,128)(2,1)}, u32[]{:S(2)}) copy-start(bf16[4,1024]{1,0:T(4,128)(2,1)} %param.21) | copy-start | bytes 24580
  11.6 13.2 %copy-start.14 = (bf16[2048,16]{0,1:T(8,128)(2,1)S(1)}, bf16[2048,16]{0,1:T(8,128)(2,1)}, u32[]{:S(2)}) copy-start(bf16[2048,16]{0,1:T(8,128)(2,1)} %param.22) | copy-start | bytes 196612
  11.6 13.2 %copy-start.15 = (bf16[16,256]{1,0:T(8,128)(2,1)S(1)}, bf16[16,256]{1,0:T(8,128)(2,1)}, u32[]{:S(2)}) copy-start(bf16[16,256]{1,0:T(8,128)(2,1)} %param.23) | copy-start | bytes 24580
  11.7 13.2 %copy-start.16 = (f32[256]{0:T(256)S(1)}, f32[256]{0:T(256)}, u32[]{:S(2)}) copy-start(f32[256]{0:T(256)} %param.24) | copy-start | bytes 3076
  18.9 1.3 copy-start.7
  20.3 25.7 %collective-permute-start = (bf16[3,1024]{1,0:T(4,128)(2,1)S(1)}, bf16[3,1024]{1,0:T(4,128)(2,1)S(1)}, u32[]{:S(2)}, u32[]{:S(2)}) collective-permute-start(bf16[3,1024]{1,0:T(4,128)(2,1)S(1)} %slice_bitcast_fusion.5), channel_id=1, source_target_pairs={{0,2},{2,4},{4,6},{1,3},{3,5},{5,7},{8,10},{10,12},{12,14},{9,11},... | collective-permute-start | bytes 18440 | tf_op jit(solution)/shard_map/ppermute | solution.py:20
  30.0 9.0 %copy-start.12 = (bf16[512]{0:T(512)(128)(2,1)S(1)}, bf16[512]{0:T(512)(128)(2,1)}, u32[]{:S(2)}) copy-start(bf16[512]{0:T(512)(128)(2,1)} %param.26) | copy-start | bytes 3076
  31.9 60.4 %copy-start.5 = (f32[16,1,64,256]{3,0,1,2:T(8,128)}, f32[16,1,64,256]{3,0,1,2:T(8,128)S(1)}, u32[]{:S(2)}) copy-start(f32[16,1,64,256]{3,0,1,2:T(8,128)S(1)} %fusion.48) | copy-start | bytes 3145732
  53.7 7.4 %copy-start.3 = (f32[16,64,1,1024]{3,1,0,2:T(8,128)}, f32[16,64,1,1024]{3,1,0,2:T(8,128)S(1)}, u32[]{:S(2)}) copy-start(f32[16,64,1,1024]{3,1,0,2:T(8,128)S(1)} %fusion.15) | copy-start | bytes 12582916
  74.7 3.2 copy-start.2
  79.3 83.3 %all-reduce.3.cloned.1.call-start = ((), (), s32[]{:S(2)}) async-start(), calls=%async_computation.2 | async-start | bytes 8388608 | tf_op jit(solution)/shard_map/psum | solution.py:203
  79.5 4.2 %copy-start.4 = (f32[16,64,1,1024]{3,1,0,2:T(8,128)S(1)}, f32[16,64,1,1024]{3,1,0,2:T(8,128)}, u32[]{:S(2)}) copy-start(f32[16,64,1,1024]{3,1,0,2:T(8,128)} %copy-done.3) | copy-start | bytes 12582916
  122.9 2.1 copy-start.10
  122.9 66.5 %all-gather.7.cloned.1.call-start = ((), (), s32[]{:S(2)}) async-start(), calls=%async_computation.3 | async-start | bytes 6127616 | tf_op jit(solution)/shard_map/all_gather | solution.py:211
  123.5 131.4 %all-gather.11.cloned.1.call-start = ((), (), s32[]{:S(2)}) async-start(), calls=%async_computation.5 | async-start | bytes 6127616 | tf_op jit(solution)/shard_map/all_gather | solution.py:216
  124.1 192.1 %all-gather.9.cloned.1.call-start = ((), (), s32[]{:S(2)}) async-start(), calls=%async_computation.4 | async-start | bytes 6127616 | tf_op jit(solution)/shard_map/all_gather | solution.py:212
  124.7 227.5 %reduce-scatter.2.cloned.1.call-start = ((), (), s32[]{:S(2)}) async-start(), calls=%async_computation.6 | async-start | bytes 6291456 | tf_op jit(solution)/shard_map/reduce_scatter | solution.py:219
  342.9 13.7 %copy-start.1 = (bf16[512,2048]{1,0:T(8,128)(2,1)S(1)}, bf16[512,2048]{1,0:T(8,128)(2,1)}, u32[]{:S(2)}) copy-start(bf16[512,2048]{1,0:T(8,128)(2,1)} %param.27) | copy-start | bytes 6291460
Sparse Core Ops, SparseCore 0:
  79.4 24.9 all-gather.4
  123.0 39.5 all-reduce.2
  337.2 14.9 reduce-scatter.1
Sparse Core Ops, SparseCore 1:
  125.7 63.6 all-gather.6
  191.6 63.2 all-gather.10
  257.1 59.0 all-gather.8

commit v2 on v1

--- a/solution.py
+++ b/solution.py
@@ -154,6 +154,10 @@
         page_count, PAGE, local_heads, CONVW
     )
     query_rows, key_rows, value_matrix = split_features(mixed_rows, HK)
+    gate_rows = lax.all_gather(gate_weight, "req", axis=0, tiled=True)
+    up_rows = lax.all_gather(up_weight, "req", axis=0, tiled=True)
+    down_columns = lax.all_gather(down_weight, "req", axis=1, tiled=True)
+    gate_rows, query_rows = lax.optimization_barrier((gate_rows, query_rows))
     lowrank = jnp.dot(normed, decay_down, preferred_element_type=jnp.float32).astype(jnp.bfloat16)
     decay_log = (
         jax.nn.log_sigmoid(
@@ -189,6 +193,7 @@
     memories = (
         memories + (alive_mask[:, None, None] * jnp.exp(through))[..., None] * incoming_state[None]
     )
+    up_rows, outputs = lax.optimization_barrier((up_rows, outputs))
     attended = outputs.transpose(0, 2, 1, 3).reshape(token_count, local_heads, HV)
     normed_heads = rms_scaled(attended, head_gain)
     opening = jax.nn.silu(jnp.dot(normed, output_gate, preferred_element_type=jnp.float32)).reshape(
@@ -197,6 +202,7 @@
     gated_rows = (
         (normed_heads * opening).astype(jnp.bfloat16).reshape(token_count, local_heads * HV)
     )
+    down_columns, gated_rows = lax.optimization_barrier((down_columns, gated_rows))
     partial_value = jnp.dot(gated_rows, output_weight, preferred_element_type=jnp.float32)
     half_rows = token_count // lax.axis_size("hid")
     row_start = lax.axis_index("hid") * half_rows
@@ -208,14 +214,10 @@
     def widen(weight_rows):
         return jnp.dot(feed_in, weight_rows, preferred_element_type=jnp.float32)
 
-    gate_part = widen(lax.all_gather(gate_weight, "req", axis=0, tiled=True))
-    up_part = widen(lax.all_gather(up_weight, "req", axis=0, tiled=True))
+    gate_part = widen(gate_rows)
+    up_part = widen(up_rows)
     hidden = (jax.nn.silu(gate_part) * up_part).astype(jnp.bfloat16)
-    partials = jnp.dot(
-        hidden,
-        lax.all_gather(down_weight, "req", axis=1, tiled=True),
-        preferred_element_type=jnp.float32,
-    )
+    partials = jnp.dot(hidden, down_columns, preferred_element_type=jnp.float32)
     feed_sum = lax.psum_scatter(
         partials.astype(jnp.bfloat16), "hid", scatter_dimension=0, tiled=True
     ).astype(jnp.float32)

time: 371 us -> 398 us (1.073)
  waiting for transfers between devices: 178 us -> 203 us
  other arithmetic: 39.8 us -> 45.1 us
  matrix products: 104 us -> 100 us
    all_gather x3, waiting for transfers between devices: 134 us -> 157 us  [the longest x1 62 us: on_device(): gate_rows = lax.all_gather(gate_weight, 'req', axis=0, tiled=True)]
    all_gather x1, waiting for transfers between devices: 0.01 us -> 4.1 us  [prefix_2(): lax.all_gather(a.astype(kind), axis)]
    unnamed x37 -> x43, local copies, waits for them, and re-layouts: 10.1 us -> 12.8 us
    reduce_sum x2 -> x3, other arithmetic: 10.9 us -> 10.5 us  [rms_scaled(): jnp.mean(values * values, axis=-1, keepdims=True) + EPSILON]
  transfers between devices with their start and end apart: 7 -> 7, of which waited for: 5 -> 6; matrix products, arithmetic and copies ran while one was open for 19% -> 17% of each run, Pallas kernels for 0% -> 0%
where the time goes in v2:
time: 398 us; the launch traced here: 392 us
  waiting for transfers between devices  203 us (51%)
  matrix products  100 us (25%)
  other arithmetic  45.1 us (11%)
  local copies, waits for them, and re-layouts  17 us (4%)
  between operations  15 us (4%)
  blocking collectives  6.9 us (2%)
  starting transfers between devices  4.61 us (1%)
    all_gather x1, waiting for transfers between devices, on_device(): gate_rows = lax.all_gather(gate_weight, 'req', axis=0, tiled=True)  62 us
    all_gather x1, waiting for transfers between devices, on_device(): down_columns = lax.all_gather(down_weight, 'req', axis=1, tiled=True)  56.9 us
    all_gather x1, waiting for transfers between devices, on_device(): up_rows = lax.all_gather(up_weight, 'req', axis=0, tiled=True)  38 us
    psum x1, waiting for transfers between devices, on_device(): lax.psum(partial_value.astype(jnp.bfloat16), 'hid').astype(jnp.float32)  34.2 us
    dot_general x1, matrix products, on_device(): partials = jnp.dot(hidden, down_columns, preferred_element_type=jnp.float32)  20.9 us
    dot_general x1, matrix products, page_block(): jnp.einsum('pqhe,qheb->pheb', weights, page_terms, precision=TOP_PRECISION)  13.6 us
    unnamed x43, local copies, waits for them, and re-layouts  12.8 us
    dot_general x1, matrix products, widen(): return jnp.dot(feed_in, weight_rows, preferred_element_type=jnp.float32)  10.7 us
  transfers between devices with their start and end apart: 7, of which 6 were waited for; matrix products, arithmetic and copies ran while one was open for 17% of the time, Pallas kernels for 0%

profile of v2, /device:TPU:1, one launch (start us, length us, event | category | flops | bytes accessed | tf_op | source)
XLA Modules:
  0.0 392.0 jit_solution(12662995687886767372)
XLA Ops:
  10.8 7.3 %convolution_convert_fusion.2 = bf16[1024,1024]{1,0:T(8,128)(2,1)S(1)} fusion(bf16[2048,1024]{1,0:T(8,128)(2,1)} %param.20, bf16[1024,2048]{1,0:T(8,128)(2,1)S(1)} %copy-done.7, f32[2048]{0:T(1024)S(1)} %convert_element_type.149, f32[1024]{0:T(1024)S(1)} %add_rsqrt_fusion.2), kind=kOutput, calls=%fused_computation.53 | convolution fusion | flops 4304404480 | bytes 10498048 | tf_op jit(solution)/shard_map/dot_general | solution.py:147
  19.4 4.4 %collective-permute-start = (bf16[3,1024]{1,0:T(4,128)(2,1)S(1)}, bf16[3,1024]{1,0:T(4,128)(2,1)S(1)}, u32[]{:S(2)}, u32[]{:S(2)}) collective-permute-start(bf16[3,1024]{1,0:T(4,128)(2,1)S(1)} %slice_bitcast_fusion.5), channel_id=1, source_target_pairs={{0,2},{2,4},{4,6},{1,3},{3,5},{5,7},{8,10},{10,12},{12,14},{9,11},... | collective-permute-start | bytes 18440 | tf_op jit(solution)/shard_map/ppermute | solution.py:20
  24.0 5.2 %fusion.37 = f32[1024,256]{1,0:T(8,128)} fusion(bf16[16,256]{1,0:T(8,128)(2,1)S(1)} %copy-done.18, bf16[2048,16]{0,1:T(8,128)(2,1)S(1)} %copy-done.17, f32[256]{0:T(256)S(1)} %copy-done.19, bf16[1024,2048]{1,0:T(8,128)(2,1)} %param.18, f32[2048]{0:T(1024)S(1)} %convert_element_type.149, f32[1024]{0:T(1024)S(1)} %add_rsqrt_fusion.2), kind=kOutput, calls=%fused_computation.60 | convolution fusion | flops 86523904 | bytes 5329920 | tf_op jit(solution)/shard_map/dot_general | solution.py:164
  32.6 4.1 %convert_element_type.152 = f32[16,64,1024]{2,1,0:T(8,128)} convert(bf16[16,64,1024]{2,1,0:T(8,128)(2,1)} %bitcast.123) | non-fusion elementwise | flops 1048576 | bytes 6291456 | tf_op jit(solution)/shard_map/convert_element_type | solution.py:65
  36.9 7.6 %fusion.15 = f32[16,64,1,1024]{3,1,0,2:T(8,128)S(1)} fusion(f32[16,64,1024]{2,1,0:T(8,128)} %convert_element_type.152, f32[16,3,1024]{2,1,0:T(4,128)S(1)} %convert_multiply_fusion.4, f32[1024]{0:T(1024)S(1)} %bitcast.130, f32[1024]{0:T(1024)S(1)} %bitcast.131, f32[1024]{0:T(1024)S(1)} %bitcast.129, f32[1024]{0:T(1024)S(1)} %bitcast.128), kind=kLoop, calls=%fused_computation.29 | loop fusion | flops 10485760 | bytes 8601600 | tf_op jit(solution)/shard_map/reshape | solution.py:153
  44.6 7.4 %fusion.30 = f32[16,256,512]{2,1,0:T(8,128)S(1)} fusion(f32[16,64,1,1024]{3,1,0,2:T(8,128)S(1)} %fusion.15, f32[16,1,64,256]{3,0,1,2:T(8,128)S(1)} %fusion.49, f32[16,256]{1,0:T(8,128)S(1)} %get-tuple-element.97), kind=kOutput, calls=%fused_computation.51 | convolution fusion | flops 1612447744 | bytes 12599296 | tf_op jit(solution)/shard_map/phte,phtb->pheb/dot_general | solution.py:101
  52.0 13.6 %fusion.20 = f32[16,1,256,512]{3,0,2,1:T(8,128)S(1)} fusion(f32[16,256,512]{2,1,0:T(8,128)S(1)} %fusion.30, f32[16,256]{0,1:T(8,128)S(1)} %bitcast.125, pred[16,16]{1,0:T(8,128)(4,1)S(1)} %fusion.72), kind=kOutput, calls=%fused_computation.38 | convolution fusion | flops 402849792 | bytes 16793856 | tf_op jit(solution)/shard_map/pqhe,qheb->pheb/dot_general | solution.py:111
  73.7 6.9 %all_gather.20 = bf16[4,1,256]{2,1,0:T(2,128)(2,1)S(1)} all-gather(bf16[1,1,256]{2,1,0:T(2,128)(2,1)S(1)} %fusion.74), channel_id=1, replica_groups=mesh['req'=16,'seq'=4,'hid'=2] {'seq'}, dimensions={0}, use_global_device_ids=true | all-gather | bytes 2560 | tf_op jit(solution)/shard_map/all_gather | solution.py:26
  83.1 8.6 %multiply_bitcast_fusion = f32[16,256,512]{2,0,1:T(8,128)} fusion(f32[15,1,256,512]{3,0,2,1:T(8,128)} %bitcast.119, f32[16]{0:T(128)S(1)} %get-tuple-element.95), kind=kLoop, calls=%fused_computation.19 | loop fusion | flops 2097152 | bytes 16252992 | tf_op jit(solution)/shard_map/reshape.33
  91.7 4.1 %all-gather.11.cloned.1.call-done = bf16[4,1,256,512]{3,2,1,0:T(8,128)(2,1)} async-done(((bf16[1,1,256,512]{3,2,1,0:T(8,128)(2,1)}), bf16[4,1,256,512]{3,2,1,0:T(8,128)(2,1)}) %all-gather.11.cloned.1.call-update) | async-done | bytes 1048592 | tf_op jit(solution)/shard_map/all_gather | solution.py:26
  96.0 62.0 %all-gather.9.cloned.1.call-done = bf16[2048,1408]{1,0:T(8,128)(2,1)} async-done(((bf16[128,1408]{1,0:T(8,128)(2,1)}), bf16[2048,1408]{1,0:T(8,128)(2,1)}) %all-gather.9.cloned.1.call-update) | async-done | bytes 5767184 | tf_op jit(solution)/shard_map/all_gather | solution.py:157
  158.0 4.7 %convolution_select_fusion = f32[16,64,64]{2,1,0:T(8,128)S(1)} fusion(f32[16,1,64,256]{3,2,0,1:T(8,128)} %multiply_bitcast_fusion.1, f32[16,1,64,256]{3,0,1,2:T(8,128)} %copy-done.5, pred[64,64]{1,0:T(8,128)(4,1)S(1)} %iota_compare_fusion, f32[16,64,1,1024]{3,1,0,2:T(8,128)} %copy-done.4), kind=kOutput, calls=%fused_computation.56 | convolution fusion | flops 203489280 | bytes 4460544 | tf_op jit(solution)/shard_map/phik,phjk->phij/dot_general | solution.py:94
  166.2 10.6 %fusion.7 = f32[16,64,512]{2,1,0:T(8,128)S(1)} fusion(f32[16,256,512]{2,0,1:T(8,128)S(1)} %copy-done.3, f32[16,1,64,256]{3,2,0,1:T(8,128)S(1)} %copy-done.8, f32[16,1,64,256]{3,0,1,2:T(8,128)S(1)} %copy-done.6), kind=kOutput, calls=%fused_computation.14 | convolution fusion | flops 1610874880 | bytes 12582912 | tf_op jit(solution)/shard_map/phik,phkv->phiv/dot_general | solution.py:114
  180.6 38.0 %all-gather.7.cloned.1.call-done = bf16[2048,1408]{1,0:T(8,128)(2,1)} async-done(((bf16[128,1408]{1,0:T(8,128)(2,1)}), bf16[2048,1408]{1,0:T(8,128)(2,1)}) %all-gather.7.cloned.1.call-update) | async-done | bytes 5767184 | tf_op jit(solution)/shard_map/all_gather | solution.py:158
  220.5 7.1 %fusion.25 = bf16[1024,512]{1,0:T(8,128)(2,1)} fusion(f32[16,1,64,512]{3,2,0,1:T(8,128)} %bitcast_add_fusion, f32[512]{0:T(512)S(1)} %convert_element_type.163, f32[1024]{0:T(1024)S(1)} %rsqrt.29, bf16[2048,512]{1,0:T(8,128)(2,1)} %param.25, bf16[1024,2048]{1,0:T(8,128)(2,1)} %param.18, f32[2048]{0:T(1024)S(1)} %convert_element_type.149, ...), kind=kOutput, calls=%fused_computation.45 | convolution fusion | flops 2160066560 | bytes 9455616 | tf_op jit(solution)/shard_map/dot_general | solution.py:199
  227.6 56.9 %all-gather.5.cloned.1.call-done = bf16[1408,2048]{1,0:T(8,128)(2,1)} async-done(((bf16[1408,128]{1,0:T(8,128)(2,1)}), bf16[1408,2048]{1,0:T(8,128)(2,1)}) %all-gather.5.cloned.1.call-update) | async-done | bytes 5767184 | tf_op jit(solution)/shard_map/all_gather | solution.py:159
  284.5 5.6 %convolution_convert_fusion.1 = bf16[1024,2048]{1,0:T(8,128)(2,1)} fusion(bf16[1024,512]{1,0:T(8,128)(2,1)} %fusion.25, bf16[512,2048]{1,0:T(8,128)(2,1)S(1)} %copy-done), kind=kOutput, calls=%fused_computation.37 | convolution fusion | flops 2149580800 | bytes 7340032 | tf_op jit(solution)/shard_map/dot_general | solution.py:206
  290.8 34.2 %all-reduce.3.cloned.1.call-done = bf16[1024,2048]{1,0:T(8,128)(2,1)} async-done(((bf16[1024,2048]{1,0:T(8,128)(2,1)}), bf16[1024,2048]{1,0:T(8,128)(2,1)}) %all-reduce.3.cloned.1.call-update) | async-done | bytes 4194320 | tf_op jit(solution)/shard_map/psum | solution.py:209
  325.0 5.5 %fusion = (f32[1024]{0:T(1024)S(1)}, bf16[1024,2048]{1,0:T(8,128)(2,1)S(1)}) fusion(bf16[1024,2048]{1,0:T(8,128)(2,1)} %all-reduce.3.cloned.1.call-done, bf16[1024,2048]{1,0:T(8,128)(2,1)} %param.18), kind=kLoop, calls=%fused_computation.7 | loop fusion | flops 14679040 | bytes 12587008 | tf_op jit(solution)/shard_map/reduce_sum | solution.py:47
  332.5 10.7 %fusion.34 = f32[1024,1408]{1,0:T(8,128)} fusion(bf16[2048,1408]{1,0:T(8,128)(2,1)} %all-gather.9.cloned.1.call-done, bf16[1024,2048]{1,0:T(8,128)(2,1)S(1)} %get-tuple-element.93, f32[2048]{0:T(1024)S(1)} %convert_element_type.170, f32[1024]{0:T(1024)S(1)} %add_rsqrt_fusion.1), kind=kOutput, calls=%fused_computation.57 | convolution fusion | flops 5913968640 | bytes 15740928 | tf_op jit(solution)/shard_map/dot_general | solution.py:215
  343.2 20.9 %convolution_convert_fusion = bf16[1024,2048]{1,0:T(8,128)(2,1)} fusion(bf16[1408,2048]{1,0:T(8,128)(2,1)} %all-gather.5.cloned.1.call-done, f32[1024,1408]{1,0:T(8,128)} %fusion.34, bf16[2048,1408]{1,0:T(8,128)(2,1)} %all-gather.7.cloned.1.call-done, bf16[1024,2048]{1,0:T(8,128)(2,1)} %copy-done.9, f32[2048]{0:T(1024)S(1)} %convert_element_type.170, ...), kind=kOutput, calls=%fused_computation.36 | convolution fusion | flops 11830296576 | bytes 25702400 | tf_op jit(solution)/shard_map/dot_general | solution.py:220
  370.0 4.5 %copy.75 = bf16[16,1,256,512]{3,2,1,0:T(8,128)(2,1)} copy(bf16[16,1,256,512]{3,0,2,1:T(8,128)(2,1)S(1)} %add_convert_fusion) | data formatting | bytes 8388608
  374.5 5.8 %reduce-scatter.2.cloned.1.call-done = bf16[512,2048]{1,0:T(8,128)(2,1)} async-done(((bf16[1024,2048]{1,0:T(8,128)(2,1)}), bf16[512,2048]{1,0:T(8,128)(2,1)}) %reduce-scatter.2.cloned.1.call-update) | async-done | bytes 2097168 | tf_op jit(solution)/shard_map/reduce_scatter | solution.py:221
  380.3 4.4 %add_convert_fusion.1 = bf16[512,2048]{1,0:T(8,128)(2,1)} fusion(bf16[512,2048]{1,0:T(8,128)(2,1)} %reduce-scatter.2.cloned.1.call-done, bf16[1024,2048]{1,0:T(8,128)(2,1)} %copy-done.9, s32[]{:T(128)S(6)} %select_n.46), kind=kLoop, calls=%fused_computation.35 | loop fusion | flops 4194304 | bytes 6291460 | tf_op jit(solution)/shard_map/convert_element_type | solution.py:224
  (98 shorter events, 37.1 us)
Async XLA Ops:
  7.2 277.4 %copy-start = (bf16[512,2048]{1,0:T(8,128)(2,1)S(1)}, bf16[512,2048]{1,0:T(8,128)(2,1)}, u32[]{:S(2)}) copy-start(bf16[512,2048]{1,0:T(8,128)(2,1)} %param.27) | copy-start | bytes 6291460
  7.2 3.3 copy-start.12
  7.2 88.6 %all-gather.11.cloned.1.call-start = ((), (), s32[]{:S(2)}) async-start(), calls=%async_computation.4 | async-start | bytes 1310720 | tf_op jit(solution)/shard_map/all_gather | solution.py:26
  7.2 3.6 copy-start.7
  10.8 13.0 %copy-start.14 = (s32[1,16]{1,0:T(1,128)S(1)}, s32[1,16]{1,0:T(1,128)}, u32[]{:S(2)}) copy-start(s32[1,16]{1,0:T(1,128)} %param.33) | copy-start | bytes 196
  10.8 13.0 %copy-start.16 = (s32[1,16]{1,0:T(1,128)S(1)}, s32[1,16]{1,0:T(1,128)}, u32[]{:S(2)}) copy-start(s32[1,16]{1,0:T(1,128)} %param.32) | copy-start | bytes 196
  10.8 13.2 %copy-start.11 = (bf16[4,1024]{1,0:T(4,128)(2,1)S(1)}, bf16[4,1024]{1,0:T(4,128)(2,1)}, u32[]{:S(2)}) copy-start(bf16[4,1024]{1,0:T(4,128)(2,1)} %param.21) | copy-start | bytes 24580
  10.8 13.2 %copy-start.17 = (bf16[2048,16]{0,1:T(8,128)(2,1)S(1)}, bf16[2048,16]{0,1:T(8,128)(2,1)}, u32[]{:S(2)}) copy-start(bf16[2048,16]{0,1:T(8,128)(2,1)} %param.22) | copy-start | bytes 196612
  10.8 13.2 %copy-start.18 = (bf16[16,256]{1,0:T(8,128)(2,1)S(1)}, bf16[16,256]{1,0:T(8,128)(2,1)}, u32[]{:S(2)}) copy-start(bf16[16,256]{1,0:T(8,128)(2,1)} %param.23) | copy-start | bytes 24580
  10.8 13.2 %copy-start.19 = (f32[256]{0:T(256)S(1)}, f32[256]{0:T(256)}, u32[]{:S(2)}) copy-start(f32[256]{0:T(256)} %param.24) | copy-start | bytes 3076
  19.4 17.3 %collective-permute-start = (bf16[3,1024]{1,0:T(4,128)(2,1)S(1)}, bf16[3,1024]{1,0:T(4,128)(2,1)S(1)}, u32[]{:S(2)}, u32[]{:S(2)}) collective-permute-start(bf16[3,1024]{1,0:T(4,128)(2,1)S(1)} %slice_bitcast_fusion.5), channel_id=1, source_target_pairs={{0,2},{2,4},{4,6},{1,3},{3,5},{5,7},{8,10},{10,12},{12,14},{9,11},... | collective-permute-start | bytes 18440 | tf_op jit(solution)/shard_map/ppermute | solution.py:20
  31.0 13.5 %copy-start.5 = (f32[16,1,64,256]{3,0,1,2:T(8,128)}, f32[16,1,64,256]{3,0,1,2:T(8,128)S(1)}, u32[]{:S(2)}) copy-start(f32[16,1,64,256]{3,0,1,2:T(8,128)S(1)} %fusion.49) | copy-start | bytes 3145732
  44.6 7.4 %copy-start.4 = (f32[16,64,1,1024]{3,1,0,2:T(8,128)}, f32[16,64,1,1024]{3,1,0,2:T(8,128)S(1)}, u32[]{:S(2)}) copy-start(f32[16,64,1,1024]{3,1,0,2:T(8,128)S(1)} %fusion.15) | copy-start | bytes 12582916
  52.0 21.1 %copy-start.15 = (bf16[512]{0:T(512)(128)(2,1)S(1)}, bf16[512]{0:T(512)(128)(2,1)}, u32[]{:S(2)}) copy-start(bf16[512]{0:T(512)(128)(2,1)} %param.26) | copy-start | bytes 3076
  65.6 3.2 copy-start.2
  70.1 87.9 %all-gather.9.cloned.1.call-start = ((), (), s32[]{:S(2)}) async-start(), calls=%async_computation.3 | async-start | bytes 6127616 | tf_op jit(solution)/shard_map/all_gather | solution.py:157
  70.9 147.7 %all-gather.7.cloned.1.call-start = ((), (), s32[]{:S(2)}) async-start(), calls=%async_computation.2 | async-start | bytes 6127616 | tf_op jit(solution)/shard_map/all_gather | solution.py:158
  71.6 212.9 %all-gather.5.cloned.1.call-start = ((), (), s32[]{:S(2)}) async-start(), calls=%async_computation.1 | async-start | bytes 6127616 | tf_op jit(solution)/shard_map/all_gather | solution.py:159
  72.2 252.8 %all-reduce.3.cloned.1.call-start = ((), (), s32[]{:S(2)}) async-start(), calls=%async_computation.5 | async-start | bytes 8388608 | tf_op jit(solution)/shard_map/psum | solution.py:209
  158.0 8.2 %copy-start.3 = (f32[16,256,512]{2,0,1:T(8,128)S(1)}, f32[16,256,512]{2,0,1:T(8,128)}, u32[]{:S(2)}) copy-start(f32[16,256,512]{2,0,1:T(8,128)} %multiply_bitcast_fusion) | copy-start | bytes 25165828
  158.0 8.2 %copy-start.6 = (f32[16,1,64,256]{3,0,1,2:T(8,128)S(1)}, f32[16,1,64,256]{3,0,1,2:T(8,128)}, u32[]{:S(2)}) copy-start(f32[16,1,64,256]{3,0,1,2:T(8,128)} %copy-done.5) | copy-start | bytes 3145732
  158.0 8.2 %copy-start.8 = (f32[16,1,64,256]{3,2,0,1:T(8,128)S(1)}, f32[16,1,64,256]{3,2,0,1:T(8,128)}, u32[]{:S(2)}) copy-start(f32[16,1,64,256]{3,2,0,1:T(8,128)} %multiply_bitcast_fusion.1) | copy-start | bytes 3145732
  290.2 90.2 %reduce-scatter.2.cloned.1.call-start = ((), (), s32[]{:S(2)}) async-start(), calls=%async_computation.6 | async-start | bytes 6291456 | tf_op jit(solution)/shard_map/reduce_scatter | solution.py:221
  370.0 14.8 %copy-start.1 = (bf16[512,2048]{1,0:T(8,128)(2,1)S(1)}, bf16[512,2048]{1,0:T(8,128)(2,1)}, u32[]{:S(2)}) copy-start(bf16[512,2048]{1,0:T(8,128)(2,1)} %param.27) | copy-start | bytes 6291460
  (3 other events, 4.0 us)
Sparse Core Ops, SparseCore 0:
  70.2 25.4 all-gather.10
  97.9 60.0 all-gather.8
  160.1 58.4 all-gather.6
  220.6 63.9 all-gather.4
  290.3 34.7 all-reduce.2
  364.2 16.0 reduce-scatter.1

commit v3 on v1

--- a/solution.py
+++ b/solution.py
@@ -1,7 +1,11 @@
+import functools
+
 import jax
 import jax.numpy as jnp
 from jax import lax
 from jax.sharding import PartitionSpec as P
+from jax.experimental import pallas as pl
+from jax.experimental.pallas import tpu as pltpu
 
 HK = 256
 HV = 512
@@ -38,6 +42,37 @@
         )
 
     return lax.fori_loop(0, place, one, state)
+
+
+def partner_kernel(rows, src_ref, dst_ref, send_sem, recv_sem):
+    partner = 1 - lax.axis_index("hid")
+    barrier = pltpu.get_barrier_semaphore()
+    pl.semaphore_signal(
+        barrier, inc=1, device_id={"hid": partner}, device_id_type=pl.DeviceIdType.MESH
+    )
+    pl.semaphore_wait(barrier, 1)
+    start = pl.multiple_of(partner * rows, rows) if rows < src_ref.shape[0] else 0
+    copy = pltpu.make_async_remote_copy(
+        src_ref=src_ref.at[pl.ds(start, rows)],
+        dst_ref=dst_ref,
+        send_sem=send_sem,
+        recv_sem=recv_sem,
+        device_id={"hid": partner},
+        device_id_type=pl.DeviceIdType.MESH,
+    )
+    copy.start()
+    copy.wait()
+
+
+def from_partner(value, rows, kernel_id):
+    return pl.pallas_call(
+        functools.partial(partner_kernel, rows),
+        out_shape=jax.ShapeDtypeStruct((rows,) + value.shape[1:], value.dtype),
+        in_specs=[pl.BlockSpec(memory_space=pl.ANY)],
+        out_specs=pl.BlockSpec(memory_space=pl.ANY),
+        scratch_shapes=[pltpu.SemaphoreType.DMA, pltpu.SemaphoreType.DMA],
+        compiler_params=pltpu.CompilerParams(collective_id=kernel_id, has_side_effects=True),
+    )(value)
 
 
 def rms_scaled(values, scale_gain):
@@ -200,7 +235,10 @@
     partial_value = jnp.dot(gated_rows, output_weight, preferred_element_type=jnp.float32)
     half_rows = token_count // lax.axis_size("hid")
     row_start = lax.axis_index("hid") * half_rows
-    mixed_sum = lax.psum(partial_value.astype(jnp.bfloat16), "hid").astype(jnp.float32)
+    own_value = partial_value.astype(jnp.bfloat16)
+    mixed_sum = own_value.astype(jnp.float32) + from_partner(own_value, token_count, 0).astype(
+        jnp.float32
+    )
     residual = (tokens.astype(jnp.float32) + mixed_sum).astype(jnp.bfloat16)
     feed_in = rms_scaled(residual, mixer_gain).astype(jnp.bfloat16)
     own_residual = lax.dynamic_slice_in_dim(residual, row_start, half_rows, 0)
@@ -216,9 +254,10 @@
         lax.all_gather(down_weight, "req", axis=1, tiled=True),
         preferred_element_type=jnp.float32,
     )
-    feed_sum = lax.psum_scatter(
-        partials.astype(jnp.bfloat16), "hid", scatter_dimension=0, tiled=True
-    ).astype(jnp.float32)
+    own_partials = partials.astype(jnp.bfloat16)
+    feed_sum = lax.dynamic_slice_in_dim(own_partials, row_start, half_rows, 0).astype(
+        jnp.float32
+    ) + from_partner(own_partials, half_rows, 1).astype(jnp.float32)
     result = (own_residual.astype(jnp.float32) + feed_sum).astype(jnp.bfloat16)
     return (result, memories.astype(jnp.bfloat16), by_page[:, PAGE - rim_rows :])
 

time: 371 us -> 330 us (0.89)
  waiting for transfers between devices: 178 us -> 122 us
  Pallas kernels: 0 us -> 15 us
  matrix products: 104 us -> 108 us
    psum x1 -> x0, waiting for transfers between devices: 37.7 us -> none  [on_device(): lax.psum(partial_value.astype(jnp.bfloat16), 'hid').astype(jnp.float32)]
    pallas_call x0 -> x2, Pallas kernels: none -> 15 us  [from_partner(): pl.pallas_call(functools.partial(partner_kernel, rows), out_shape=jax.Sha...]
    all_gather x1, waiting for transfers between devices: 19.1 us -> 5.25 us  [on_device(): gate_part = widen(lax.all_gather(gate_weight, 'req', axis=0, tiled=True))]
    reduce_scatter x1 -> x0, waiting for transfers between devices: 4.81 us -> none  [on_device(): lax.psum_scatter(partials.astype(jnp.bfloat16), 'hid', scatter_dimension=...]
    reduce_sum x2, other arithmetic: 10.9 us -> 7.13 us  [rms_scaled(): jnp.mean(values * values, axis=-1, keepdims=True) + EPSILON]
    unnamed x37 -> x45, local copies, waits for them, and re-layouts: 10.1 us -> 10.1 us
  transfers between devices with their start and end apart: 7 -> 5, of which waited for: 5 -> 3; matrix products, arithmetic and copies ran while one was open for 19% -> 27% of each run, Pallas kernels for 0% -> 3%
where the time goes in v3:
time: 330 us; the launch traced here: 323 us
  waiting for transfers between devices  122 us (37%)
  matrix products  108 us (33%)
  other arithmetic  37.4 us (11%)
  Pallas kernels  15 us (5%)
  between operations  14.6 us (4%)
  local copies, waits for them, and re-layouts  14.5 us (4%)
  blocking collectives  7.07 us (2%)
  starting transfers between devices  4.53 us (1%)
    all_gather x1, waiting for transfers between devices, on_device(): up_part = widen(lax.all_gather(up_weight, 'req', axis=0, tiled=True))  61.1 us
    all_gather x1, waiting for transfers between devices, on_device(): lax.all_gather(down_weight, 'req', axis=1, tiled=True)  54.2 us
    dot_general x1, matrix products, on_device(): jnp.dot(hidden, lax.all_gather(down_weight, 'req', axis=1, tiled=True), p...  20.9 us
    dot_general x1, matrix products, page_block(): jnp.einsum('phik,phkv->phiv', raised_rows, previous, precision=TOP_PRECIS...  15.4 us
    pallas_call x2, Pallas kernels, from_partner(): pl.pallas_call(functools.partial(partner_kernel, rows), out_shape=jax.Sha...  15 us
    dot_general x1, matrix products, page_block(): jnp.einsum('pqhe,qheb->pheb', weights, page_terms, precision=TOP_PRECISION)  13.6 us
    dot_general x1, matrix products, widen(): return jnp.dot(feed_in, weight_rows, preferred_element_type=jnp.float32)  11.9 us
    unnamed x45, local copies, waits for them, and re-layouts  10.1 us
  transfers between devices with their start and end apart: 5, of which 3 were waited for; matrix products, arithmetic and copies ran while one was open for 27% of the time, Pallas kernels for 3%

profile of v3, /device:TPU:1, one launch (start us, length us, event | category | flops | bytes accessed | tf_op | source)
XLA Modules:
  0.0 323.4 jit_solution(3893730658220096074)
XLA Ops:
  10.8 7.3 %convolution_convert_fusion.2 = bf16[1024,1024]{1,0:T(8,128)(2,1)S(1)} fusion(bf16[2048,1024]{1,0:T(8,128)(2,1)} %param.20, bf16[1024,2048]{1,0:T(8,128)(2,1)S(1)} %copy-done.5, f32[2048]{0:T(1024)S(1)} %convert_element_type.155, f32[1024]{0:T(1024)S(1)} %add_rsqrt_fusion.2), kind=kOutput, calls=%fused_computation.53 | convolution fusion | flops 4304404480 | bytes 10498048 | tf_op jit(solution)/shard_map/dot_general | solution.py:182
  19.4 4.4 %collective-permute-start = (bf16[3,1024]{1,0:T(4,128)(2,1)S(1)}, bf16[3,1024]{1,0:T(4,128)(2,1)S(1)}, u32[]{:S(2)}, u32[]{:S(2)}) collective-permute-start(bf16[3,1024]{1,0:T(4,128)(2,1)S(1)} %slice_bitcast_fusion.5), channel_id=1, source_target_pairs={{0,2},{2,4},{4,6},{1,3},{3,5},{5,7},{8,10},{10,12},{12,14},{9,11},... | collective-permute-start | bytes 18440 | tf_op jit(solution)/shard_map/ppermute | solution.py:24
  24.0 5.2 %fusion.37 = f32[1024,256]{1,0:T(8,128)} fusion(bf16[16,256]{1,0:T(8,128)(2,1)S(1)} %copy-done.17, bf16[2048,16]{0,1:T(8,128)(2,1)S(1)} %copy-done.16, f32[256]{0:T(256)S(1)} %copy-done.18, bf16[1024,2048]{1,0:T(8,128)(2,1)} %param.18, f32[2048]{0:T(1024)S(1)} %convert_element_type.155, f32[1024]{0:T(1024)S(1)} %add_rsqrt_fusion.2), kind=kOutput, calls=%fused_computation.60 | convolution fusion | flops 86523904 | bytes 5329920 | tf_op jit(solution)/shard_map/dot_general | solution.py:195
  36.9 7.6 %fusion.15 = f32[16,64,1,1024]{3,1,0,2:T(8,128)S(1)} fusion(f32[16,64,1024]{2,1,0:T(8,128)} %convert_element_type.158, f32[16,3,1024]{2,1,0:T(4,128)S(1)} %convert_multiply_fusion.4, f32[1024]{0:T(1024)S(1)} %bitcast.147, f32[1024]{0:T(1024)S(1)} %bitcast.148, f32[1024]{0:T(1024)S(1)} %bitcast.146, f32[1024]{0:T(1024)S(1)} %bitcast.145), kind=kLoop, calls=%fused_computation.29 | loop fusion | flops 10485760 | bytes 8601600 | tf_op jit(solution)/shard_map/reshape | solution.py:188
  44.6 7.4 %fusion.30 = f32[16,256,512]{2,1,0:T(8,128)S(1)} fusion(f32[16,64,1,1024]{3,1,0,2:T(8,128)S(1)} %fusion.15, f32[16,1,64,256]{3,0,1,2:T(8,128)S(1)} %fusion.48, f32[16,256]{1,0:T(8,128)S(1)} %get-tuple-element.85), kind=kOutput, calls=%fused_computation.51 | convolution fusion | flops 1612447744 | bytes 12599296 | tf_op jit(solution)/shard_map/phte,phtb->pheb/dot_general | solution.py:136
  52.0 13.6 %fusion.20 = f32[16,1,256,512]{3,0,2,1:T(8,128)S(1)} fusion(f32[16,256,512]{2,1,0:T(8,128)S(1)} %fusion.30, f32[16,256]{0,1:T(8,128)S(1)} %bitcast.142, pred[16,16]{1,0:T(8,128)(4,1)S(1)} %fusion.69), kind=kOutput, calls=%fused_computation.38 | convolution fusion | flops 402849792 | bytes 16793856 | tf_op jit(solution)/shard_map/pqhe,qheb->pheb/dot_general | solution.py:146
  75.7 7.1 %all_gather.17 = bf16[4,1,256]{2,1,0:T(2,128)(2,1)S(1)} all-gather(bf16[1,1,256]{2,1,0:T(2,128)(2,1)S(1)} %fusion.71), channel_id=1, replica_groups=mesh['req'=16,'seq'=4,'hid'=2] {'seq'}, dimensions={0}, use_global_device_ids=true | all-gather | bytes 2560 | tf_op jit(solution)/shard_map/all_gather | solution.py:30
  82.8 4.2 %convolution_select_fusion = f32[16,64,64]{2,1,0:T(8,128)S(1)} fusion(f32[16,1,64,256]{3,0,1,2:T(8,128)S(1)} %fusion.48, pred[64,64]{1,0:T(8,128)(4,1)S(1)} %iota_compare_fusion, f32[16,64,1,1024]{3,1,0,2:T(8,128)} %copy-done.3), kind=kOutput, calls=%fused_computation.56 | convolution fusion | flops 204537856 | bytes 4464640 | tf_op jit(solution)/shard_map/phik,phjk->phij/dot_general | solution.py:129
  87.0 4.7 %fusion.31 = f32[16,64,512]{2,1,0:T(8,128)} fusion(f32[16,64,64]{2,1,0:T(8,128)S(1)} %convolution_select_fusion, f32[16,64,1,1024]{3,1,0,2:T(8,128)} %copy-done.3), kind=kOutput, calls=%fused_computation.52 | convolution fusion | flops 402653184 | bytes 4456448 | tf_op jit(solution)/shard_map/phij,phjv->phiv/dot_general | solution.py:133
  91.7 5.0 %multiply_bitcast_fusion = f32[16,256,512]{2,0,1:T(8,128)} fusion(f32[15,1,256,512]{3,0,2,1:T(8,128)S(1)} %bitcast.136, f32[16]{0:T(128)S(1)} %get-tuple-element.83), kind=kLoop, calls=%fused_computation.19 | loop fusion | flops 2097152 | bytes 16252992 | tf_op jit(solution)/shard_map/reshape.33
  96.7 15.4 %fusion.7 = f32[16,64,512]{2,1,0:T(8,128)} fusion(f32[16,256,512]{2,0,1:T(8,128)} %multiply_bitcast_fusion, f32[16,1,64,256]{3,0,1,2:T(8,128)S(1)} %fusion.48, f32[16,64,1,1024]{3,1,0,2:T(8,128)} %copy-done.3), kind=kOutput, calls=%fused_computation.14 | convolution fusion | flops 1611923456 | bytes 12582912 | tf_op jit(solution)/shard_map/phik,phkv->phiv/dot_general | solution.py:149
  112.3 6.8 %multiply_reduce_fusion = (f32[16,64]{1,0:T(8,128)S(1)}, f32[16,1,64,512]{3,2,0,1:T(8,128)}) fusion(f32[16,1,64,256]{3,0,1,2:T(8,128)} %copy-done.4, f32[16,256]{1,0:T(8,128)S(1)} %get-tuple-element.84, f32[16]{0:T(128)S(1)} %reduce.3, f32[16,64,1,1024]{3,1,0,2:T(8,128)} %copy-done.3, f32[1,256,512]{2,1,0:T(8,128)S(1)} %get-tuple-element.47, ...), kind=kOutput, calls=%fused_computation.46 | convolution fusion | flops 1614543872 | bytes 8933440 | tf_op jit(solution)/shard_map/dlof,lfg->dlog/dot_general | solution.py:221
  119.2 6.2 %fusion.25 = bf16[1024,512]{1,0:T(8,128)(2,1)S(1)} fusion(f32[16,1,64,512]{3,2,0,1:T(8,128)} %get-tuple-element.91, f32[512]{0:T(512)S(1)} %convert_element_type.169, f32[1024]{0:T(1024)S(1)} %rsqrt.29, bf16[2048,512]{1,0:T(8,128)(2,1)} %param.25, bf16[1024,2048]{1,0:T(8,128)(2,1)} %param.18, f32[2048]{0:T(1024)S(1)} %convert_element_type.155, ...), kind=kOutput, calls=%fused_computation.45 | convolution fusion | flops 2160066560 | bytes 9455616 | tf_op jit(solution)/shard_map/dot_general | solution.py:229
  125.4 4.3 %convolution_convert_fusion.1.src_ref = bf16[1024,2048]{1,0:T(8,128)(2,1)} fusion(bf16[1024,512]{1,0:T(8,128)(2,1)S(1)} %fusion.25, bf16[512,2048]{1,0:T(8,128)(2,1)S(1)} %copy-done), kind=kOutput, calls=%fused_computation.37 | convolution fusion | flops 2149580800 | bytes 7340032 | tf_op jit(solution)/shard_map/dot_general | solution.py:235
  129.7 10.1 %shard_map.175 = bf16[1024,2048]{1,0:T(8,128)(2,1)} custom-call(bf16[1024,2048]{1,0:T(8,128)(2,1)} %convolution_convert_fusion.1.src_ref), custom_call_target="tpu_custom_call" | custom-call | tf_op jit(solution)/shard_map/pallas_call | solution.py:68
  139.9 4.5 %add_convert_fusion = bf16[16,1,256,512]{3,0,2,1:T(8,128)(2,1)S(1)} fusion(f32[16,1,256,512]{3,0,2,1:T(8,128)} %copy-done.2, f32[256,512]{1,0:T(8,128)S(1)} %bitcast.137, f32[16,256]{0,1:T(8,128)S(1)} %copy.70), kind=kLoop, calls=%fused_computation.18 | loop fusion | flops 6291456 | bytes 13123584 | tf_op jit(solution)/shard_map/convert_element_type | solution.py:262
  144.4 4.4 %copy.71 = bf16[16,1,256,512]{3,2,1,0:T(8,128)(2,1)} copy(bf16[16,1,256,512]{3,0,2,1:T(8,128)(2,1)S(1)} %add_convert_fusion) | data formatting | bytes 8388608
  152.8 5.3 %all-gather.7.cloned.1.call-done = bf16[2048,1408]{1,0:T(8,128)(2,1)} async-done(((bf16[128,1408]{1,0:T(8,128)(2,1)}), bf16[2048,1408]{1,0:T(8,128)(2,1)}) %all-gather.7.cloned.1.call-update) | async-done | bytes 5767184 | tf_op jit(solution)/shard_map/all_gather | solution.py:249
  158.0 11.9 %fusion.34 = f32[1024,1408]{1,0:T(8,128)} fusion(bf16[2048,1408]{1,0:T(8,128)(2,1)} %all-gather.7.cloned.1.call-done, bf16[1024,2048]{1,0:T(8,128)(2,1)} %get-tuple-element.81, f32[2048]{0:T(1024)S(1)} %convert_element_type.177, f32[1024]{0:T(1024)S(1)} %add_rsqrt_fusion.1), kind=kOutput, calls=%fused_computation.57 | convolution fusion | flops 5913968640 | bytes 15740928 | tf_op jit(solution)/shard_map/dot_general | solution.py:247
  169.9 54.2 %all-gather.11.cloned.1.call-done = bf16[1408,2048]{1,0:T(8,128)(2,1)} async-done(((bf16[1408,128]{1,0:T(8,128)(2,1)}), bf16[1408,2048]{1,0:T(8,128)(2,1)}) %all-gather.11.cloned.1.call-update) | async-done | bytes 5767184 | tf_op jit(solution)/shard_map/all_gather | solution.py:254
  224.1 61.1 %all-gather.9.cloned.1.call-done = bf16[2048,1408]{1,0:T(8,128)(2,1)} async-done(((bf16[128,1408]{1,0:T(8,128)(2,1)}), bf16[2048,1408]{1,0:T(8,128)(2,1)}) %all-gather.9.cloned.1.call-update) | async-done | bytes 5767184 | tf_op jit(solution)/shard_map/all_gather | solution.py:250
  285.1 20.9 %convolution_convert_fusion.src_ref = bf16[1024,2048]{1,0:T(8,128)(2,1)} fusion(bf16[1408,2048]{1,0:T(8,128)(2,1)} %all-gather.11.cloned.1.call-done, f32[1024,1408]{1,0:T(8,128)} %fusion.34, bf16[2048,1408]{1,0:T(8,128)(2,1)} %all-gather.9.cloned.1.call-done, bf16[1024,2048]{1,0:T(8,128)(2,1)} %get-tuple-element.81, f32[2048]{0:T(1024)S(1)} %convert_element_type.177, ...), kind=kOutput, calls=%fused_computation.36 | convolution fusion | flops 11830296576 | bytes 25702400 | tf_op jit(solution)/shard_map/dot_general | solution.py:252
  306.0 4.8 %shard_map.176 = bf16[512,2048]{1,0:T(8,128)(2,1)} custom-call(bf16[1024,2048]{1,0:T(8,128)(2,1)} %convolution_convert_fusion.src_ref), custom_call_target="tpu_custom_call" | custom-call | tf_op jit(solution)/shard_map/pallas_call | solution.py:68
  310.9 5.6 %add_convert_fusion.1 = bf16[512,2048]{1,0:T(8,128)(2,1)} fusion(bf16[512,2048]{1,0:T(8,128)(2,1)} %shard_map.176, bf16[1024,2048]{1,0:T(8,128)(2,1)} %convolution_convert_fusion.src_ref, s32[]{:T(128)S(6)} %select_n.47, bf16[1024,2048]{1,0:T(8,128)(2,1)} %get-tuple-element.81), kind=kLoop, calls=%fused_computation.35 | loop fusion | flops 6291456 | bytes 8388612 | tf_op jit(solution)/shard_map/convert_element_type | solution.py:261
  (95 shorter events, 26.8 us)
Async XLA Ops:
  7.2 118.2 %copy-start = (bf16[512,2048]{1,0:T(8,128)(2,1)S(1)}, bf16[512,2048]{1,0:T(8,128)(2,1)}, u32[]{:S(2)}) copy-start(bf16[512,2048]{1,0:T(8,128)(2,1)} %param.27) | copy-start | bytes 6291460
  7.2 3.3 %copy-start.11 = (bf16[2048]{0:T(1024)(128)(2,1)S(1)}, bf16[2048]{0:T(1024)(128)(2,1)}, u32[]{:S(2)}) copy-start(bf16[2048]{0:T(1024)(128)(2,1)} %param.19) | copy-start | bytes 12292
  7.2 105.0 %all-gather.5.cloned.1.call-start = ((), (), s32[]{:S(2)}) async-start(), calls=%async_computation | async-start | bytes 1310720 | tf_op jit(solution)/shard_map/all_gather | solution.py:30
  7.2 3.6 %copy-start.5 = (bf16[1024,2048]{1,0:T(8,128)(2,1)S(1)}, bf16[1024,2048]{1,0:T(8,128)(2,1)}, u32[]{:S(2)}) copy-start(bf16[1024,2048]{1,0:T(8,128)(2,1)} %param.18) | copy-start | bytes 12582916
  10.8 13.0 %copy-start.13 = (s32[1,16]{1,0:T(1,128)S(1)}, s32[1,16]{1,0:T(1,128)}, u32[]{:S(2)}) copy-start(s32[1,16]{1,0:T(1,128)} %param.33) | copy-start | bytes 196
  10.8 13.0 %copy-start.15 = (s32[1,16]{1,0:T(1,128)S(1)}, s32[1,16]{1,0:T(1,128)}, u32[]{:S(2)}) copy-start(s32[1,16]{1,0:T(1,128)} %param.32) | copy-start | bytes 196
  10.8 13.2 %copy-start.10 = (bf16[4,1024]{1,0:T(4,128)(2,1)S(1)}, bf16[4,1024]{1,0:T(4,128)(2,1)}, u32[]{:S(2)}) copy-start(bf16[4,1024]{1,0:T(4,128)(2,1)} %param.21) | copy-start | bytes 24580
  10.8 13.2 %copy-start.16 = (bf16[2048,16]{0,1:T(8,128)(2,1)S(1)}, bf16[2048,16]{0,1:T(8,128)(2,1)}, u32[]{:S(2)}) copy-start(bf16[2048,16]{0,1:T(8,128)(2,1)} %param.22) | copy-start | bytes 196612
  10.8 13.2 %copy-start.17 = (bf16[16,256]{1,0:T(8,128)(2,1)S(1)}, bf16[16,256]{1,0:T(8,128)(2,1)}, u32[]{:S(2)}) copy-start(bf16[16,256]{1,0:T(8,128)(2,1)} %param.23) | copy-start | bytes 24580
  10.8 13.2 %copy-start.18 = (f32[256]{0:T(256)S(1)}, f32[256]{0:T(256)}, u32[]{:S(2)}) copy-start(f32[256]{0:T(256)} %param.24) | copy-start | bytes 3076
  19.4 17.3 %collective-permute-start = (bf16[3,1024]{1,0:T(4,128)(2,1)S(1)}, bf16[3,1024]{1,0:T(4,128)(2,1)S(1)}, u32[]{:S(2)}, u32[]{:S(2)}) collective-permute-start(bf16[3,1024]{1,0:T(4,128)(2,1)S(1)} %slice_bitcast_fusion.5), channel_id=1, source_target_pairs={{0,2},{2,4},{4,6},{1,3},{3,5},{5,7},{8,10},{10,12},{12,14},{9,11},... | collective-permute-start | bytes 18440 | tf_op jit(solution)/shard_map/ppermute | solution.py:24
  31.0 65.7 %copy-start.4 = (f32[16,1,64,256]{3,0,1,2:T(8,128)}, f32[16,1,64,256]{3,0,1,2:T(8,128)S(1)}, u32[]{:S(2)}) copy-start(f32[16,1,64,256]{3,0,1,2:T(8,128)S(1)} %fusion.48) | copy-start | bytes 3145732
  44.6 7.4 %copy-start.3 = (f32[16,64,1,1024]{3,1,0,2:T(8,128)}, f32[16,64,1,1024]{3,1,0,2:T(8,128)S(1)}, u32[]{:S(2)}) copy-start(f32[16,64,1,1024]{3,1,0,2:T(8,128)S(1)} %fusion.15) | copy-start | bytes 12582916
  52.0 22.1 %copy-start.14 = (bf16[512]{0:T(512)(128)(2,1)S(1)}, bf16[512]{0:T(512)(128)(2,1)}, u32[]{:S(2)}) copy-start(bf16[512]{0:T(512)(128)(2,1)} %param.26) | copy-start | bytes 3076
  52.0 22.1 %copy-start.12 = (bf16[2048]{0:T(1024)(128)(2,1)S(1)}, bf16[2048]{0:T(1024)(128)(2,1)}, u32[]{:S(2)}) copy-start(bf16[2048]{0:T(1024)(128)(2,1)} %param.28) | copy-start | bytes 12292
  70.1 87.9 %all-gather.7.cloned.1.call-start = ((), (), s32[]{:S(2)}) async-start(), calls=%async_computation.1 | async-start | bytes 6127616 | tf_op jit(solution)/shard_map/all_gather | solution.py:249
  70.9 153.2 %all-gather.11.cloned.1.call-start = ((), (), s32[]{:S(2)}) async-start(), calls=%async_computation.3 | async-start | bytes 6127616 | tf_op jit(solution)/shard_map/all_gather | solution.py:254
  71.6 213.5 %all-gather.9.cloned.1.call-start = ((), (), s32[]{:S(2)}) async-start(), calls=%async_computation.2 | async-start | bytes 6127616 | tf_op jit(solution)/shard_map/all_gather | solution.py:250
  82.8 9.0 %slice-start = ((s8[8388608]{0:T(1024)(128)(4,1)}), s8[4194304]{0:T(1024)(128)(4,1)S(1)}, s32[]{:S(2)}) async-start(s8[8388608]{0:T(1024)(128)(4,1)} %bitcast.134), calls=%async_computation.4 | async-start | bytes 8388608
  82.8 9.0 %slice-start.1 = ((s8[8388608]{0:T(1024)(128)(4,1)}), s8[4194304]{0:T(1024)(128)(4,1)S(1)}, s32[]{:S(2)}) async-start(s8[8388608]{0:T(1024)(128)(4,1)} %bitcast.134), calls=%async_computation.5 | async-start | bytes 8388608
  139.8 9.0 %copy-start.8 = (bf16[1024,2048]{1,0:T(8,128)(2,1)S(1)}, bf16[1024,2048]{1,0:T(8,128)(2,1)}, u32[]{:S(2)}) copy-start(bf16[1024,2048]{1,0:T(8,128)(2,1)} %shard_map.175) | copy-start | bytes 12582916
  144.4 4.4 %copy-start.6 = (bf16[1024,2048]{1,0:T(8,128)(2,1)S(1)}, bf16[1024,2048]{1,0:T(8,128)(2,1)}, u32[]{:S(2)}) copy-start(bf16[1024,2048]{1,0:T(8,128)(2,1)} %param.18) | copy-start | bytes 12582916
  144.4 4.4 %copy-start.7 = (bf16[1024,2048]{1,0:T(8,128)(2,1)S(1)}, bf16[1024,2048]{1,0:T(8,128)(2,1)}, u32[]{:S(2)}) copy-start(bf16[1024,2048]{1,0:T(8,128)(2,1)} %convolution_convert_fusion.1.src_ref) | copy-start | bytes 12582916
  306.0 10.5 %copy-start.1 = (bf16[512,2048]{1,0:T(8,128)(2,1)S(1)}, bf16[512,2048]{1,0:T(8,128)(2,1)}, u32[]{:S(2)}) copy-start(bf16[512,2048]{1,0:T(8,128)(2,1)} %param.27) | copy-start | bytes 6291460
  (2 other events, 4.5 us)
Sparse Core Ops, SparseCore 0:
  70.3 25.4 all-gather.4
  97.9 60.0 all-gather.6
  160.1 63.9 all-gather.10
  226.1 59.0 all-gather.8
